TPU v7x, 32 devices: a whole 2x2x4 slice. The times are simulated.
32 devices in a mesh: region: 8 (over z, core), member: 4 (over y, x).
Axes of the slice: x: 2, y: 2, z: 4, core: 2. Of those that a mesh axis runs over, the one named last changes fastest.
Arguments:
- positions: float32 [3, 12288], P(None, ('region', 'member'))
- forces: float32 [3, 12288], P(None, ('region', 'member')), may hold values from -6 to 6
- blob_platelet: int32 [12288], P(('region', 'member')), may hold values from 0 to 8, as said below
- blob_rank: int32 [12288], P(('region', 'member')), may hold values from 0 to 161, as said below
- platelet_owner: int32 [64], P('region'), may hold values from 0 to 7, as said below
- pair_list: int32 [96, 8], P(('region', 'member')), may hold values from 0 to 23, as said below
- pair_count: int32 [96], P(('region', 'member')), may hold values from 1 to 8, as said below
- preconditioner: bfloat16 [64, 486, 486], P(('region', 'member')), may hold values from -0.25 to 0.25
Outputs:
- blob_velocity: float32 [3, 12288], P(None, ('region', 'member'))
- body_velocity: float32 [64, 486], P(('region', 'member'))
Inputs may be any that keep to these rules, and one draw needn't show every extreme that they name: `blob_platelet`: in each slab every platelet id below 8 appears on exactly 162 slots, and 8 marks an empty slot. Every device holds exactly 324 live blobs, of which at most 121 belong to platelets whose owner slots lie on one member; that bound is met in every slab. `blob_rank`: the 162 blobs of one platelet have distinct ranks; empty slots have rank 0. `platelet_owner`: the 8 entries of one slab are a permutation; owner slot o lies on member o // 2 of that slab. `pair_list`: the entries of one target tile are distinct, and entry 0 is the tile itself, 6 plus its index within its slab. `pair_count`: some tile has 8 in every draw.
All inputs are finite; a program needn't handle non-finite values.
Results may differ from a plain program's by a relative error of at most 0.0029.
Values sent between devices are 32-bit elements; how exact they have to be, the bound alone decides.
A program may use at most 64 MiB of HBM per device.

v0:
```python
import functools
import math

import jax
import jax.numpy as jnp
from jax import lax
from jax.experimental import pallas as pl
from jax.experimental.pallas import tpu as pltpu
from jax.sharding import PartitionSpec as P

TILE = 128
SUB = 8
VROWS = 4
SCALE = 1.0 / (8.0 * math.pi)
MESH = pl.DeviceIdType.MESH


def pair_terms(x1, x2, x3, src):
    y1, y2, h, f1, f2, f3, h2 = src
    d1 = x1 - y1
    d2 = x2 - y2
    d3 = x3 - h
    r3 = x3 + h
    s = d1 * d1 + d2 * d2
    w = lax.rsqrt(s + d3 * d3 + 1.0)
    p = lax.rsqrt(s + r3 * r3)
    w3 = w * w * w
    p2 = p * p
    p3 = p2 * p
    along = d1 * f1 + d2 * f2
    full = along + d3 * f3
    mirror = along - r3 * f3
    cp3 = (h2 * x3) * p3
    alpha = (w + w3) - (p + cp3)
    gamma = 3.0 * (cp3 * p2) * mirror
    both = full * (w3 - p3) + gamma
    return (
        f1 * alpha + d1 * both,
        f2 * alpha + d2 * both,
        f3 * alpha + d3 * both + h2 * gamma,
    )


def kernel(
    n_region,
    n_member,
    pb,
    own_plates,
    pos_hbm,
    force_hbm,
    plate_hbm,
    rank_hbm,
    owner_hbm,
    list_hbm,
    count_hbm,
    vel_out,
    body_out,
    pos,
    force,
    plate,
    rank,
    owner_ref,
    list_ref,
    count_ref,
    ext,
    tgt,
    acc,
    vel,
    hot,
    in_sem,
    send_sem,
    recv_sem,
    vsend_sem,
    vrecv_sem,
):
    r = lax.axis_index("region")
    m = lax.axis_index("member")
    half = n_member // 2
    tiles = pos.shape[1] // TILE
    blobs = pos.shape[1]
    plates = owner_ref.shape[0]
    pairs = list_ref.shape[1]
    has_low = r > 0
    has_high = r < n_region - 1
    to_high = jnp.logical_and(m >= half, has_high)
    to_low = jnp.logical_and(m < half, has_low)

    loads = [
        pltpu.make_async_copy(a, b, in_sem.at[i])
        for i, (a, b) in enumerate(
            ((pos_hbm, pos), (force_hbm, force), (plate_hbm, plate.at[0]), (rank_hbm, rank.at[0]),
             (owner_hbm, owner_ref), (list_hbm, list_ref), (count_hbm, count_ref))
        )
    ]
    for load in loads:
        load.start()

    barrier = pltpu.get_barrier_semaphore()
    for step in range(1, n_member):
        pl.semaphore_signal(
            barrier, inc=1, device_id=(r, lax.rem(m + step, n_member)), device_id_type=MESH
        )

    @pl.when(has_low)
    def _():
        for k in range(half):
            pl.semaphore_signal(barrier, inc=1, device_id=(r - 1, half + k), device_id_type=MESH)

    @pl.when(has_high)
    def _():
        for k in range(half):
            pl.semaphore_signal(barrier, inc=1, device_id=(r + 1, k), device_id_type=MESH)

    for load in loads:
        load.wait()

    base = (half + m) * tiles
    plate_row = plate[...]
    rank_row = rank[...]
    live = plate_row < plates
    slot_of = jnp.zeros_like(plate_row)
    for k in range(plates):
        slot_of = jnp.where(plate_row == k, owner_ref[k], slot_of)
    body_at = jnp.where(live, slot_of * pb + rank_row, plates * pb).astype(jnp.float32)
    live_f = live.astype(jnp.float32)
    packed = jnp.concatenate(
        [pos[...], force[...] * live_f, body_at, jnp.zeros_like(body_at)], axis=0
    )
    for t in range(tiles):
        ext[base + t] = packed[:, t * TILE : (t + 1) * TILE]

    @pl.when(jnp.logical_not(has_low))
    def _():
        ext[pl.ds(0, half * tiles)] = jnp.zeros((half * tiles, SUB, TILE), jnp.float32)

    @pl.when(jnp.logical_not(has_high))
    def _():
        ext[pl.ds((half + n_member) * tiles, half * tiles)] = jnp.zeros(
            (half * tiles, SUB, TILE), jnp.float32
        )

    for t in range(tiles):
        for c in range(3):
            row = packed[c : c + 1, t * TILE : (t + 1) * TILE]
            tgt[t * 3 + c] = jnp.broadcast_to(row, (TILE, TILE)).T

    def block(e):
        return ext.at[pl.ds(e * tiles, tiles)]

    def near_copy(step):
        return pltpu.make_async_remote_copy(
            src_ref=block(half + m),
            dst_ref=block(half + m),
            send_sem=send_sem.at[step],
            recv_sem=recv_sem.at[half + m],
            device_id=(r, lax.rem(m + step, n_member)),
            device_id_type=MESH,
        )

    def rim_copy(k, shift, e):
        return pltpu.make_async_remote_copy(
            src_ref=block(half + m),
            dst_ref=block(e),
            send_sem=send_sem.at[n_member + k],
            recv_sem=recv_sem.at[e],
            device_id=(r + shift, lax.rem(m + k, n_member)),
            device_id_type=MESH,
        )

    def arrival(e):
        return pltpu.make_async_remote_copy(
            src_ref=block(e),
            dst_ref=block(e),
            send_sem=send_sem.at[0],
            recv_sem=recv_sem.at[e],
            device_id=(r, lax.rem(m + 1, n_member)),
            device_id_type=MESH,
        )

    rim_sends = jnp.where(jnp.logical_or(to_high, to_low), n_member, 0)
    pl.semaphore_wait(barrier, n_member - 1 + rim_sends)

    @pl.when(to_high)
    def _():
        for k in range(n_member):
            rim_copy(k, 1, m - half).start()

    @pl.when(to_low)
    def _():
        for k in range(n_member):
            rim_copy(k, -1, half + n_member + m).start()

    for step in range(1, n_member):
        near_copy(step).start()

    def one_pair(t, s, tile_id, first):
        keep = jnp.where(s < count_ref[t], SCALE, 0.0)
        rows = ext[tile_id]

        def wide(c):
            return jnp.broadcast_to(rows[c : c + 1], (SUB, TILE))

        h = wide(2)
        src = (wide(0), wide(1), h, wide(3) * keep, wide(4) * keep, wide(5) * keep, h + h)
        for b in range(TILE // SUB):
            at = pl.ds(b * SUB, SUB)
            terms = pair_terms(tgt[t * 3, at], tgt[t * 3 + 1, at], tgt[t * 3 + 2, at], src)
            for c in range(3):
                if first:
                    acc[t * 3 + c, at] = terms[c]
                else:
                    acc[t * 3 + c, at] = acc[t * 3 + c, at] + terms[c]

    @pl.loop(0, tiles)
    def _(t):
        one_pair(t, 0, base + t, True)

    for step in range(1, n_member):
        arrival(half + lax.rem(m + step, n_member)).wait_recv()

    @pl.when(has_low)
    def _():
        for k in range(half):
            arrival(k).wait_recv()

    @pl.when(has_high)
    def _():
        for k in range(half):
            arrival(half + n_member + k).wait_recv()

    zeros = jnp.zeros((VROWS - 3, TILE), jnp.float32)

    def vel_copy(t, step, at):
        part = vel.at[:, pl.ds(pl.multiple_of(at * blobs + t * TILE, TILE), TILE)]
        return pltpu.make_async_remote_copy(
            src_ref=part,
            dst_ref=part,
            send_sem=vsend_sem.at[t, step],
            recv_sem=vrecv_sem.at[t, at],
            device_id=(r, lax.rem(m + step, n_member)),
            device_id_type=MESH,
        )

    @pl.loop(0, tiles)
    def _(t):
        for s in range(1, pairs):
            one_pair(t, s, list_ref[t, s], False)

    for t in range(tiles):
        rows = [jnp.sum(acc[t * 3 + c].T, axis=0, keepdims=True) for c in range(3)]
        at = pl.multiple_of(m * blobs + t * TILE, TILE)
        vel[:, pl.ds(at, TILE)] = jnp.concatenate(rows + [zeros], axis=0)
        vel_out[:, t * TILE : (t + 1) * TILE] = jnp.concatenate(rows, axis=0)
        for step in range(1, n_member):
            vel_copy(t, step, m).start()

    width = hot.shape[0] // own_plates
    place = lax.broadcasted_iota(jnp.int32, (hot.shape[0], TILE), 0)

    @pl.loop(0, n_member * tiles)
    def _(i):
        local = ext[half * tiles + i][6:7].astype(jnp.int32) - m * (own_plates * pb)
        row = jnp.full_like(local, -1)
        for k in range(own_plates):
            inside = jnp.logical_and(local >= k * pb, local < (k + 1) * pb)
            row = jnp.where(inside, local + k * (width - pb), row)
        at = pl.multiple_of(i * TILE, TILE)
        hot[:, pl.ds(at, TILE)] = jnp.where(place == row, 1.0, 0.0).astype(jnp.bfloat16)

    for step in range(1, n_member):
        for t in range(tiles):
            vel_copy(t, step, lax.rem(m + step, n_member)).wait_recv()

    placed = lax.dot_general(
        vel[...].astype(jnp.bfloat16),
        hot[...],
        (((1,), (1,)), ((), ())),
        preferred_element_type=jnp.float32,
    )
    order = 3 * pb
    total = 2 * width
    for k in range(own_plates):
        part = placed[:, k * width : (k + 1) * width]
        part = jnp.concatenate([part, jnp.zeros((VROWS, total - width), jnp.float32)], axis=1)
        body = part[0:1]
        for c in range(1, 3):
            body = body + pltpu.roll(part, c * pb, 1)[c : c + 1]
        body_out[k : k + 1] = body[:, :order]

    for step in range(1, n_member):
        near_copy(step).wait_send()
        for t in range(tiles):
            vel_copy(t, step, m).wait_send()

    @pl.when(to_high)
    def _():
        for k in range(n_member):
            rim_copy(k, 1, m - half).wait_send()

    @pl.when(to_low)
    def _():
        for k in range(n_member):
            rim_copy(k, -1, half + n_member + m).wait_send()


def finish(vel_ref, body_ref, vel_out, body_out):
    vel_out[...] = vel_ref[...]
    body_out[...] = body_ref[...]


def on_device(n_region, n_member, positions, forces, blob_platelet, blob_rank, owner, pair_list, pair_count, pre):
    blobs = positions.shape[1]
    tiles = blobs // TILE
    own_plates, order, _ = pre.shape
    pb = order // 3
    width = -(-pb // TILE) * TILE
    far = pl.BlockSpec(memory_space=pltpu.HBM)
    vector = pl.BlockSpec(memory_space=pltpu.VMEM)
    velocity, body_in = pl.pallas_call(
        functools.partial(kernel, n_region, n_member, pb, own_plates),
        out_shape=(
            pltpu.VMEM((3, blobs), jnp.float32),
            pltpu.VMEM((own_plates, order), jnp.float32),
        ),
        in_specs=[far] * 7,
        out_specs=(vector, vector),
        scratch_shapes=[
            pltpu.VMEM((3, blobs), jnp.float32),
            pltpu.VMEM((3, blobs), jnp.float32),
            pltpu.VMEM((1, blobs), jnp.int32),
            pltpu.VMEM((1, blobs), jnp.int32),
            pltpu.SMEM(owner.shape, jnp.int32),
            pltpu.SMEM(pair_list.shape, jnp.int32),
            pltpu.SMEM(pair_count.shape, jnp.int32),
            pltpu.VMEM((2 * n_member * tiles, SUB, TILE), jnp.float32),
            pltpu.VMEM((3 * tiles, TILE, TILE), jnp.float32),
            pltpu.VMEM((3 * tiles, TILE, TILE), jnp.float32),
            pltpu.VMEM((VROWS, n_member * blobs), jnp.float32),
            pltpu.VMEM((own_plates * width, n_member * blobs), jnp.bfloat16),
            pltpu.SemaphoreType.DMA((7,)),
            pltpu.SemaphoreType.DMA((2 * n_member,)),
            pltpu.SemaphoreType.DMA((2 * n_member,)),
            pltpu.SemaphoreType.DMA((tiles, n_member)),
            pltpu.SemaphoreType.DMA((tiles, n_member)),
        ],
        compiler_params=pltpu.CompilerParams(collective_id=0, has_side_effects=True),
    )(
        positions,
        forces,
        blob_platelet,
        blob_rank,
        owner,
        pair_list,
        pair_count,
    )
    body_velocity = jnp.einsum(
        "pab,pb->pa", pre, body_in.astype(jnp.bfloat16), preferred_element_type=jnp.float32
    )
    return pl.pallas_call(
        finish,
        out_shape=(
            jax.ShapeDtypeStruct(velocity.shape, jnp.float32),
            jax.ShapeDtypeStruct(body_velocity.shape, jnp.float32),
        ),
        in_specs=[vector, vector],
        out_specs=(vector, vector),
        compiler_params=pltpu.CompilerParams(vmem_limit_bytes=1024 * 1024),
    )(velocity, body_velocity)


def solution(mesh):
    placed = (
        P(None, ("region", "member")),
        P(None, ("region", "member")),
        P(("region", "member")),
        P(("region", "member")),
        P("region"),
        P(("region", "member"), None),
        P(("region", "member")),
        P(("region", "member"), None, None),
    )
    return jax.shard_map(
        functools.partial(on_device, mesh.shape["region"], mesh.shape["member"]),
        mesh=mesh,
        in_specs=placed,
        out_specs=(P(None, ("region", "member")), P(("region", "member"), None)),
        check_vma=False,
    )
```

profile of v0, /device:TPU:0, one launch (start us, length us, event | category | flops | bytes accessed | tf_op | source)
XLA Modules:
  0.0 15.7 jit_solution(3029437716597162874)
XLA Ops:
  0.6 0.0 copy-start
  0.6 14.0 %shard_map.95 = (f32[3,384]{1,0:T(4,128)S(1)}, f32[2,486]{1,0:T(2,128)S(1)}) custom-call(f32[3,384]{1,0:T(4,128)} %pos_hbm.1, f32[3,384]{1,0:T(4,128)} %force_hbm.1, s32[384]{0:T(512)} %plate_hbm.1, s32[384]{0:T(512)} %rank_hbm.1, s32[8]{0:T(128)} %owner_hbm.1, s32[3,8]{1,0:T(4,128)} %list_hbm.1, s32[3]{0:T(128)} %count_hbm.1), custom_call_target="tpu_custom_call" | custom-call | tf_op jit(solution)/shard_map/pallas_call | solution.py:319
  14.7 0.0 copy-done
  14.7 0.4 %fusion = f32[2,1,486]{2,1,0:T(1,128)S(1)} fusion(bf16[2,486,486]{2,0,1:T(2,128)(2,1)S(1)} %copy-done, bf16[2,486,1]{1,0,2:T(2,128)(2,1)S(1)} %convert_bitcast_fusion), kind=kOutput, calls=%fused_computation | convolution fusion | flops 944784 | bytes 950616 | tf_op jit(solution)/shard_map/pab,pb->pa/dot_general | solution.py:356
  15.1 0.6 %shard_map.96 = (f32[3,384]{1,0:T(4,128)}, f32[2,486]{1,0:T(2,128)}) custom-call(f32[3,384]{1,0:T(4,128)S(1)} %get-tuple-element.4.vel_ref, f32[2,486]{1,0:T(2,128)S(1)} %bitcast.5), custom_call_target="tpu_custom_call" | custom-call | tf_op jit(solution)/shard_map/pallas_call | solution.py:359
  (2 shorter events, 0.0 us)
Async XLA Ops:
  0.6 14.1 %copy-start = (bf16[2,486,486]{2,0,1:T(2,128)(2,1)S(1)}, bf16[2,486,486]{2,0,1:T(2,128)(2,1)}, u32[]{:S(2)}) copy-start(bf16[2,486,486]{2,0,1:T(2,128)(2,1)} %param.15) | copy-start | bytes 2834356
where the time goes:
time: 15.8 us; the launch traced here: 15.7 us
  Pallas kernels  14.6 us (92%)
  between operations  0.67 us (4%)
  matrix products  0.36 us (2%)
    pallas_call x1, Pallas kernels, on_device(): pl.pallas_call(functools.partial(kernel, n_region, n_member, pb, own_plat...  14 us
    pallas_call x1, Pallas kernels, on_device(): pl.pallas_call(finish, out_shape=(jax.ShapeDtypeStruct(velocity.shape, jn...  0.62 us
    dot_general x1, matrix products, on_device(): jnp.einsum('pab,pb->pa', pre, body_in.astype(jnp.bfloat16), preferred_ele...  0.36 us

commit v1 on v0

v1 whole, which is shorter than its diff:
```python
import functools
import math

import jax
import jax.numpy as jnp
from jax import lax
from jax.experimental import pallas as pl
from jax.experimental.pallas import tpu as pltpu
from jax.sharding import PartitionSpec as P

TILE = 128
SUB = 8
VROWS = 4
ROWS = 6
SCALE = 1.0 / (8.0 * math.pi)
MESH = pl.DeviceIdType.MESH


def pair_terms(x1, x2, x3, src):
    y1, y2, h, f1, f2, f3, h2 = src
    d1 = x1 - y1
    d2 = x2 - y2
    d3 = x3 - h
    r3 = x3 + h
    s = d1 * d1 + d2 * d2
    w = lax.rsqrt(s + d3 * d3 + 1.0)
    p = lax.rsqrt(s + r3 * r3)
    w3 = w * w * w
    p2 = p * p
    p3 = p2 * p
    along = d1 * f1 + d2 * f2
    full = along + d3 * f3
    mirror = along - r3 * f3
    cp3 = (h2 * x3) * p3
    alpha = (w + w3) - (p + cp3)
    gamma = 3.0 * (cp3 * p2) * mirror
    both = full * (w3 - p3) + gamma
    return (
        f1 * alpha + d1 * both,
        f2 * alpha + d2 * both,
        f3 * alpha + d3 * both + h2 * gamma,
    )


def kernel(
    n_region,
    n_member,
    pb,
    own_plates,
    pos_hbm,
    force_hbm,
    plate_hbm,
    rank_hbm,
    owner_hbm,
    list_hbm,
    count_hbm,
    vel_out,
    body_out,
    pos,
    force,
    plate,
    rank,
    owner_ref,
    list_ref,
    count_ref,
    ext,
    ids,
    tgt,
    acc,
    vel,
    hot,
    local_sem,
    data_sem,
    vel_sem,
):
    r = lax.axis_index("region")
    m = lax.axis_index("member")
    half = n_member // 2
    tiles = pos.shape[1] // TILE
    blobs = pos.shape[1]
    plates = owner_ref.shape[0]
    pairs = list_ref.shape[1]
    has_low = r > 0
    has_high = r < n_region - 1
    to_high = jnp.logical_and(m >= half, has_high)
    to_low = jnp.logical_and(m < half, has_low)
    base = (half + m) * tiles

    def other(step):
        return lax.rem(m + step, n_member)

    barrier = pltpu.get_barrier_semaphore()
    for step in range(1, n_member):
        pl.semaphore_signal(barrier, inc=1, device_id=(r, other(step)), device_id_type=MESH)

    loads = [
        pltpu.make_async_copy(a, b, local_sem.at[i])
        for i, (a, b) in enumerate(
            ((pos_hbm, pos), (force_hbm, force), (plate_hbm, plate.at[0]), (rank_hbm, rank.at[0]),
             (owner_hbm, owner_ref), (list_hbm, list_ref), (count_hbm, count_ref))
        )
    ]
    for load in loads[:3]:
        load.start()

    @pl.when(has_low)
    def _():
        for k in range(half):
            pl.semaphore_signal(barrier, inc=1, device_id=(r - 1, half + k), device_id_type=MESH)

    @pl.when(has_high)
    def _():
        for k in range(half):
            pl.semaphore_signal(barrier, inc=1, device_id=(r + 1, k), device_id_type=MESH)

    for load in loads[3:]:
        load.start()

    for load in loads[:3]:
        load.wait()

    live = plate[...] < plates
    place_row = pos[...]
    push_row = force[...] * live.astype(jnp.float32)
    for t in range(tiles):
        span = slice(t * TILE, (t + 1) * TILE)
        for c in range(3):
            ext[base + t, c] = place_row[c : c + 1, span]
            ext[base + t, 3 + c] = push_row[c : c + 1, span]

    def block(e, count=1):
        return ext.at[pl.ds(e * tiles, count * tiles)]

    def move(src, dst, send, recv, to):
        return pltpu.make_async_remote_copy(
            src_ref=src, dst_ref=dst, send_sem=send, recv_sem=recv, device_id=to, device_id_type=MESH
        )

    def near_copy(step):
        here = block(half + m)
        return move(here, here, local_sem.at[0], data_sem.at[0], (r, other(step)))

    def rim_copy(k, shift, e, sem):
        return move(block(half + m), block(e), local_sem.at[1], data_sem.at[sem], (r + shift, lax.rem(m + k, n_member)))

    def sized(ref, send, recv):
        return move(ref, ref, send, recv, (r, other(1)))

    rim_sends = jnp.where(jnp.logical_or(to_high, to_low), n_member, 0)
    pl.semaphore_wait(barrier, n_member - 1 + rim_sends)

    for step in range(1, n_member):
        near_copy(step).start()

    @pl.when(to_high)
    def _():
        for k in range(n_member):
            rim_copy(k, 1, m - half, 1).start()

    @pl.when(to_low)
    def _():
        for k in range(n_member):
            rim_copy(k, -1, half + n_member + m, 2).start()

    for load in loads[3:]:
        load.wait()

    plate_row = plate[...]
    slot_of = jnp.zeros_like(plate_row)
    for k in range(plates):
        slot_of = jnp.where(plate_row == k, owner_ref[k], slot_of)
    body_at = jnp.where(live, slot_of * pb + rank[...], plates * pb)
    for t in range(tiles):
        ids[m * tiles + t] = body_at[:, t * TILE : (t + 1) * TILE]

    def ids_copy(step):
        here = ids.at[pl.ds(m * tiles, tiles)]
        return move(here, here, local_sem.at[2], data_sem.at[3], (r, other(step)))

    for step in range(1, n_member):
        ids_copy(step).start()

    @pl.when(jnp.logical_not(has_low))
    def _():
        ext[pl.ds(0, half * tiles)] = jnp.zeros((half * tiles, ROWS, 1, TILE), jnp.float32)

    @pl.when(jnp.logical_not(has_high))
    def _():
        ext[pl.ds((half + n_member) * tiles, half * tiles)] = jnp.zeros(
            (half * tiles, ROWS, 1, TILE), jnp.float32
        )

    for t in range(tiles):
        for c in range(3):
            row = place_row[c : c + 1, t * TILE : (t + 1) * TILE]
            tgt[t * 3 + c] = jnp.broadcast_to(row, (TILE, TILE)).T

    def one_pair(t, s, tile_id, first):
        keep = jnp.where(s < count_ref[t], SCALE, 0.0)

        def wide(c):
            return jnp.broadcast_to(ext[tile_id, c], (SUB, TILE))

        h = wide(2)
        src = (wide(0), wide(1), h, wide(3) * keep, wide(4) * keep, wide(5) * keep, h + h)
        for b in range(TILE // SUB):
            at = pl.ds(b * SUB, SUB)
            terms = pair_terms(tgt[t * 3, at], tgt[t * 3 + 1, at], tgt[t * 3 + 2, at], src)
            for c in range(3):
                if first:
                    acc[t * 3 + c, at] = terms[c]
                else:
                    acc[t * 3 + c, at] = acc[t * 3 + c, at] + terms[c]

    @pl.loop(0, tiles)
    def _(t):
        one_pair(t, 0, base + t, True)

    sized(block(0, n_member - 1), local_sem.at[0], data_sem.at[0]).wait_recv()

    @pl.when(has_low)
    def _():
        sized(block(0, half), local_sem.at[0], data_sem.at[1]).wait_recv()

    @pl.when(has_high)
    def _():
        sized(block(0, half), local_sem.at[0], data_sem.at[2]).wait_recv()

    zeros = jnp.zeros((VROWS - 3, TILE), jnp.float32)

    def vel_copy(t, step):
        part = vel.at[m, :, pl.ds(pl.multiple_of(t * TILE, TILE), TILE)]
        return move(part, part, local_sem.at[3], vel_sem.at[m], (r, other(step)))

    @pl.loop(0, tiles)
    def _(t):
        for s in range(1, pairs):
            one_pair(t, s, list_ref[t, s], False)
        rows = [jnp.sum(acc[t * 3 + c].T, axis=0, keepdims=True) for c in range(3)]
        at = pl.ds(pl.multiple_of(t * TILE, TILE), TILE)
        vel[m, :, at] = jnp.concatenate(rows + [zeros], axis=0)
        vel_out[:, at] = jnp.concatenate(rows, axis=0)
        for step in range(1, n_member):
            vel_copy(t, step).start()

    sized(ids.at[pl.ds(0, (n_member - 1) * tiles)], local_sem.at[2], data_sem.at[3]).wait_recv()
    width = hot.shape[1] // own_plates
    place = lax.broadcasted_iota(jnp.int32, (hot.shape[1], TILE), 0)

    @pl.loop(0, n_member)
    def _(e):
        for t in range(tiles):
            local = ids[e * tiles + t] - m * (own_plates * pb)
            row = jnp.full_like(local, -1)
            for k in range(own_plates):
                inside = jnp.logical_and(local >= k * pb, local < (k + 1) * pb)
                row = jnp.where(inside, local + k * (width - pb), row)
            hot[e, :, t * TILE : (t + 1) * TILE] = jnp.where(place == row, 1.0, 0.0).astype(jnp.bfloat16)

    def placed(e):
        return lax.dot_general(
            vel[e].astype(jnp.bfloat16),
            hot[e],
            (((1,), (1,)), ((), ())),
            preferred_element_type=jnp.float32,
        )

    body_all = placed(m)
    for step in range(1, n_member):
        e = other(step)
        sized(vel.at[e], local_sem.at[3], vel_sem.at[e]).wait_recv()
        body_all = body_all + placed(e)

    order = 3 * pb
    total = 2 * width
    bodies = []
    for k in range(own_plates):
        part = body_all[:, k * width : (k + 1) * width]
        part = jnp.concatenate([part, jnp.zeros((VROWS, total - width), jnp.float32)], axis=1)
        body = part[0:1]
        for c in range(1, 3):
            body = body + pltpu.roll(part, c * pb, 1)[c : c + 1]
        bodies.append(body[:, :order])
    body_out[...] = jnp.concatenate(bodies, axis=0).astype(jnp.bfloat16)

    sized(block(0, n_member - 1), local_sem.at[0], data_sem.at[0]).wait_send()
    sized(ids.at[pl.ds(0, (n_member - 1) * tiles)], local_sem.at[2], data_sem.at[3]).wait_send()
    sized(vel.at[pl.ds(0, n_member - 1)], local_sem.at[3], vel_sem.at[0]).wait_send()

    @pl.when(jnp.logical_or(to_high, to_low))
    def _():
        sized(block(0, n_member), local_sem.at[1], data_sem.at[1]).wait_send()


def finish(vel_ref, body_ref, vel_out, body_out):
    vel_out[...] = vel_ref[...]
    body_out[...] = body_ref[...]


def on_device(n_region, n_member, positions, forces, blob_platelet, blob_rank, owner, pair_list, pair_count, pre):
    blobs = positions.shape[1]
    tiles = blobs // TILE
    own_plates, order, _ = pre.shape
    pb = order // 3
    width = -(-pb // TILE) * TILE
    far = pl.BlockSpec(memory_space=pltpu.HBM)
    vector = pl.BlockSpec(memory_space=pltpu.VMEM)
    velocity, body_in = pl.pallas_call(
        functools.partial(kernel, n_region, n_member, pb, own_plates),
        out_shape=(
            pltpu.VMEM((3, blobs), jnp.float32),
            pltpu.VMEM((own_plates, order), jnp.bfloat16),
        ),
        in_specs=[far] * 7,
        out_specs=(vector, vector),
        scratch_shapes=[
            pltpu.VMEM((3, blobs), jnp.float32),
            pltpu.VMEM((3, blobs), jnp.float32),
            pltpu.VMEM((1, blobs), jnp.int32),
            pltpu.VMEM((1, blobs), jnp.int32),
            pltpu.SMEM(owner.shape, jnp.int32),
            pltpu.SMEM(pair_list.shape, jnp.int32),
            pltpu.SMEM(pair_count.shape, jnp.int32),
            pltpu.VMEM((2 * n_member * tiles, ROWS, 1, TILE), jnp.float32),
            pltpu.VMEM((n_member * tiles, 1, TILE), jnp.int32),
            pltpu.VMEM((3 * tiles, TILE, TILE), jnp.float32),
            pltpu.VMEM((3 * tiles, TILE, TILE), jnp.float32),
            pltpu.VMEM((n_member, VROWS, blobs), jnp.float32),
            pltpu.VMEM((n_member, own_plates * width, blobs), jnp.bfloat16),
            pltpu.SemaphoreType.DMA((7,)),
            pltpu.SemaphoreType.DMA((4,)),
            pltpu.SemaphoreType.DMA((n_member,)),
        ],
        compiler_params=pltpu.CompilerParams(collective_id=0, has_side_effects=True),
    )(
        positions,
        forces,
        blob_platelet,
        blob_rank,
        owner,
        pair_list,
        pair_count,
    )
    body_velocity = jnp.einsum("pab,pb->pa", pre, body_in, preferred_element_type=jnp.float32)
    return pl.pallas_call(
        finish,
        out_shape=(
            jax.ShapeDtypeStruct(velocity.shape, jnp.float32),
            jax.ShapeDtypeStruct(body_velocity.shape, jnp.float32),
        ),
        in_specs=[vector, vector],
        out_specs=(vector, vector),
        compiler_params=pltpu.CompilerParams(vmem_limit_bytes=1024 * 1024),
    )(velocity, body_velocity)


def solution(mesh):
    placed = (
        P(None, ("region", "member")),
        P(None, ("region", "member")),
        P(("region", "member")),
        P(("region", "member")),
        P("region"),
        P(("region", "member"), None),
        P(("region", "member")),
        P(("region", "member"), None, None),
    )
    return jax.shard_map(
        functools.partial(on_device, mesh.shape["region"], mesh.shape["member"]),
        mesh=mesh,
        in_specs=placed,
        out_specs=(P(None, ("region", "member")), P(("region", "member"), None)),
        check_vma=False,
    )
```

time: 15.8 us -> 15 us (0.949)
  Pallas kernels: 14.6 us -> 13.8 us
    pallas_call x1, Pallas kernels: 14 us -> 13.2 us  [on_device(): pl.pallas_call(functools.partial(kernel, n_region, n_member, pb, own_plat...]
where the time goes in v1:
time: 15 us; the launch traced here: 14.9 us
  Pallas kernels  13.8 us (92%)
  between operations  0.66 us (4%)
  matrix products  0.36 us (2%)
    pallas_call x1, Pallas kernels, on_device(): pl.pallas_call(functools.partial(kernel, n_region, n_member, pb, own_plat...  13.2 us
    pallas_call x1, Pallas kernels, on_device(): pl.pallas_call(finish, out_shape=(jax.ShapeDtypeStruct(velocity.shape, jn...  0.62 us
    dot_general x1, matrix products, on_device(): jnp.einsum('pab,pb->pa', pre, body_in, preferred_element_type=jnp.float32)  0.36 us

profile of v1, /device:TPU:0, one launch (start us, length us, event | category | flops | bytes accessed | tf_op | source)
XLA Modules:
  0.0 14.9 jit_solution(12316277632012754810)
XLA Ops:
  0.6 0.0 copy-start
  0.6 13.2 %shard_map.95 = (f32[3,384]{1,0:T(4,128)S(1)}, bf16[2,486]{1,0:T(2,128)(2,1)S(1)}) custom-call(f32[3,384]{1,0:T(4,128)} %pos_hbm.1, f32[3,384]{1,0:T(4,128)} %force_hbm.1, s32[384]{0:T(512)} %plate_hbm.1, s32[384]{0:T(512)} %rank_hbm.1, s32[8]{0:T(128)} %owner_hbm.1, s32[3,8]{1,0:T(4,128)} %list_hbm.1, s32[3]{0:T(128)} %count_hbm.1), custom_call_target="tpu_custom_call" | custom-call | tf_op jit(solution)/shard_map/pallas_call | solution.py:308
  13.9 0.0 copy-done
  13.9 0.4 %fusion = f32[2,1,486]{2,1,0:T(1,128)S(1)} fusion(bf16[2,486,486]{2,0,1:T(2,128)(2,1)S(1)} %copy-done, bf16[2,486,1]{1,0,2:T(2,128)(2,1)S(1)} %bitcast.5), kind=kOutput, calls=%fused_computation | convolution fusion | flops 944784 | bytes 950616 | tf_op jit(solution)/shard_map/pab,pb->pa/dot_general | solution.py:344
  14.2 0.6 %shard_map.96 = (f32[3,384]{1,0:T(4,128)}, f32[2,486]{1,0:T(2,128)}) custom-call(f32[3,384]{1,0:T(4,128)S(1)} %get-tuple-element.4.vel_ref, f32[2,486]{1,0:T(2,128)S(1)} %bitcast.4), custom_call_target="tpu_custom_call" | custom-call | tf_op jit(solution)/shard_map/pallas_call | solution.py:345
  (1 shorter events, 0.0 us)
Async XLA Ops:
  0.6 13.2 %copy-start = (bf16[2,486,486]{2,0,1:T(2,128)(2,1)S(1)}, bf16[2,486,486]{2,0,1:T(2,128)(2,1)}, u32[]{:S(2)}) copy-start(bf16[2,486,486]{2,0,1:T(2,128)(2,1)} %param.15) | copy-start | bytes 2834356

commit v2 on v1

v2 whole, which is shorter than its diff:
```python
import functools
import math

import jax
import jax.numpy as jnp
from jax import lax
from jax.experimental import pallas as pl
from jax.experimental.pallas import tpu as pltpu
from jax.sharding import PartitionSpec as P

TILE = 128
SUB = 8
VROWS = 4
ROWS = 8
PLANES = 4
DEPTH = 64
GATHER = 7
SCALE = 1.0 / (8.0 * math.pi)
MESH = pl.DeviceIdType.MESH


def split3(v):
    hi = v.astype(jnp.bfloat16).astype(jnp.float32)
    rest = v - hi
    mid = rest.astype(jnp.bfloat16).astype(jnp.float32)
    return hi, mid, rest - mid


def target_table(x):
    zero = jnp.zeros((1, TILE), jnp.float32)
    one = jnp.ones((1, TILE), jnp.float32)
    squares = jnp.sum(x * x, axis=0, keepdims=True)

    def plane(rows, tail=(), fixed=None):
        parts = list(zip(*[split3(v) for v in rows]))
        fixed = (zero, zero) if fixed is None else fixed
        blocks = []
        for k, part in enumerate((0, 0, 0, 1, 1, 2)):
            blocks += list(parts[part]) + (list(fixed) if k < 3 else [zero, zero])
        tail = list(split3(tail)) if len(tail) else [zero] * 3
        blocks += tail + [zero] * (DEPTH - len(blocks) - 3)
        blocks += [zero] * (TILE - DEPTH)
        return jnp.concatenate(blocks, axis=0).T[:, :DEPTH]

    x1, x2, x3 = x[0:1], x[1:2], x[2:3]
    none = [zero] * 3
    planes = [
        plane([-2.0 * x1, -2.0 * x2, -2.0 * x3] + none, squares + 1.0, (one, zero)),
        plane([-2.0 * x1, -2.0 * x2, 2.0 * x3] + none, squares, (one, zero)),
        plane(none + [x1, x2, x3], (), (zero, -one)),
        plane(none + [3.0 * x1, 3.0 * x2, -3.0 * x3], (), (zero, -3.0 * one)),
    ]
    rows = [p[b : b + SUB] for b in range(0, TILE, SUB) for p in planes]
    return jnp.concatenate(rows, axis=0).astype(jnp.bfloat16)


def source_table(rows, middle):
    row = lax.broadcasted_iota(jnp.int32, (SUB, TILE), 0)
    near = rows - middle
    squares = near * near
    products = near * pltpu.roll(near, SUB - 3, 0)

    def summed(v, at):
        v = v + pltpu.roll(v, SUB - 1, 0) + pltpu.roll(v, SUB - 2, 0)
        return pltpu.roll(v, at, 0)

    near = jnp.where(row == 6, summed(squares, 6), jnp.where(row == 7, summed(products, 7), near))
    hi, mid, lo = split3(near)
    ones = jnp.where(row < 3, 1.0, 0.0)
    spare = jnp.zeros((DEPTH - 7 * SUB, TILE), jnp.float32)
    return jnp.concatenate([hi, mid, lo, hi, mid, hi, ones, spare], axis=0).astype(jnp.bfloat16)


def gather_table(ext, count, table):
    section = lax.broadcasted_iota(jnp.int32, (3 * ROWS, TILE), 0) % ROWS
    spare = jnp.zeros((table.shape[1] - 3 * count - 3 * ROWS, TILE), jnp.float32)
    none = jnp.zeros((3 * ROWS, TILE), jnp.float32)
    turned = []
    for p, (c, factor) in enumerate(((0, -1.0), (1, -1.0), (2, -1.0), (2, 2.0), (3, 1.0), (4, 1.0), (5, 1.0))):
        parts = split3(ext[pl.ds(0, count), c, :] * factor)
        ones = jnp.where(section == p, 1.0, 0.0) if p < 3 else none
        turned.append(jnp.concatenate([*parts, ones, spare], axis=0).T)
    rows = [v[b : b + SUB] for b in range(0, TILE, SUB) for v in turned]
    table[...] = jnp.concatenate(rows, axis=0).astype(jnp.bfloat16)


def gathered_pairs(table, count, lists, parts, x3, pairs):
    x3 = jnp.broadcast_to(x3, (SUB, TILE))
    x3d = x3 + x3
    total = [jnp.zeros((SUB, TILE), jnp.float32)] * 3
    tile = lax.broadcasted_iota(jnp.int32, (count, TILE), 0).astype(jnp.float32)
    spare = jnp.zeros((table.shape[1] - 3 * count - 3 * ROWS, TILE), jnp.float32)
    for first in range(0, pairs, 2):
        columns = []
        for s in range(first, first + 2):
            chosen = jnp.where(lists[pairs : pairs + 1] > s, lists[s : s + 1], -1.0)
            hot = jnp.where(tile == chosen, 1.0, 0.0)
            columns.append(jnp.concatenate([hot, hot, hot, *parts, spare], axis=0))
        columns = jnp.concatenate(columns, axis=1).astype(jnp.bfloat16)
        planes = jnp.dot(table[...], columns, preferred_element_type=jnp.float32)
        for side in range(2):
            for b in range(TILE // SUB):
                d1, d2, d3, h2, f1, f2, f3 = [
                    planes[(b * GATHER + p) * SUB :][:SUB, side * TILE : (side + 1) * TILE] for p in range(GATHER)
                ]
                dd = d1 * d1 + d2 * d2 + d3 * d3
                c = h2 * x3
                w = lax.rsqrt(dd + 1.0)
                p = lax.rsqrt(dd + (c + c))
                w3 = w * w * w
                p2 = p * p
                p3 = p2 * p
                full = d1 * f1 + d2 * f2 + d3 * f3
                mirror = full - x3d * f3
                cp3 = c * p3
                alpha = (w + w3) - (p + cp3)
                gamma = 3.0 * (cp3 * p2) * mirror
                both = full * (w3 - p3) + gamma
                total[0] = total[0] + (f1 * alpha + d1 * both)
                total[1] = total[1] + (f2 * alpha + d2 * both)
                total[2] = total[2] + (f3 * alpha + d3 * both + h2 * gamma)
    return [jnp.sum(v, axis=0, keepdims=True) for v in total]


def kernel(
    n_region,
    n_member,
    pb,
    own_plates,
    pos_hbm,
    force_hbm,
    plate_hbm,
    rank_hbm,
    owner_hbm,
    list_hbm,
    count_hbm,
    vel_out,
    body_out,
    pos,
    force,
    plate,
    rank,
    owner_ref,
    list_ref,
    count_ref,
    ext,
    ids,
    sources,
    targets,
    tgt,
    acc,
    table,
    vel,
    hot,
    local_sem,
    data_sem,
    vel_sem,
):
    r = lax.axis_index("region")
    m = lax.axis_index("member")
    half = n_member // 2
    tiles = pos.shape[1] // TILE
    blobs = pos.shape[1]
    plates = owner_ref.shape[0]
    pairs = list_ref.shape[1]
    has_low = r > 0
    has_high = r < n_region - 1
    to_high = jnp.logical_and(m >= half, has_high)
    to_low = jnp.logical_and(m < half, has_low)
    base = (half + m) * tiles

    far = n_member - 1 - m
    lower = jnp.where(m < half, m, far)

    def peer(j):
        mate = lax.rem(lower + 1 + j // 2, half)
        return jnp.where(j % 2 == 0, mate, n_member - 1 - mate)

    peers = [peer(j) for j in range(n_member - 2)]
    others = peers + [far]

    barrier = pltpu.get_barrier_semaphore()
    for e in others:
        pl.semaphore_signal(barrier, inc=1, device_id=(r, e), device_id_type=MESH)

    loads = [
        pltpu.make_async_copy(a, b, local_sem.at[i])
        for i, (a, b) in enumerate(
            ((pos_hbm, pos), (force_hbm, force), (plate_hbm, plate.at[0]), (rank_hbm, rank.at[0]),
             (owner_hbm, owner_ref), (list_hbm, list_ref), (count_hbm, count_ref))
        )
    ]
    for load in loads[:3]:
        load.start()

    @pl.when(has_low)
    def _():
        for k in range(half):
            pl.semaphore_signal(barrier, inc=1, device_id=(r - 1, half + k), device_id_type=MESH)

    @pl.when(has_high)
    def _():
        for k in range(half):
            pl.semaphore_signal(barrier, inc=1, device_id=(r + 1, k), device_id_type=MESH)

    for load in loads[3:]:
        load.start()

    for load in loads[:3]:
        load.wait()

    live = plate[...] < plates
    place_row = pos[...]
    push_row = force[...] * jnp.where(live, SCALE, 0.0)
    packed = jnp.concatenate([place_row, push_row, jnp.zeros((ROWS - 6, blobs), jnp.float32)], axis=0)
    for t in range(tiles):
        ext[base + t] = packed[:, t * TILE : (t + 1) * TILE]

    def block(e, count=1):
        return ext.at[pl.ds(e * tiles, count * tiles)]

    def move(src, dst, send, recv, to):
        return pltpu.make_async_remote_copy(
            src_ref=src, dst_ref=dst, send_sem=send, recv_sem=recv, device_id=to, device_id_type=MESH
        )

    def near_copy(e):
        here = block(half + m)
        return move(here, here, local_sem.at[0], data_sem.at[0], (r, e))

    def rim_copy(k, shift, e, sem):
        return move(block(half + m), block(e), local_sem.at[1], data_sem.at[sem], (r + shift, lax.rem(m + k, n_member)))

    def sized(ref, send, recv):
        return move(ref, ref, send, recv, (r, far))

    rim_sends = jnp.where(jnp.logical_or(to_high, to_low), n_member, 0)
    pl.semaphore_wait(barrier, n_member - 1 + rim_sends)

    for e in others:
        near_copy(e).start()

    @pl.when(to_high)
    def _():
        for k in range(n_member):
            rim_copy(k, 1, m - half, 1).start()

    @pl.when(to_low)
    def _():
        for k in range(n_member):
            rim_copy(k, -1, half + n_member + m, 2).start()

    for load in loads[3:]:
        load.wait()

    plate_row = plate[...]
    slot_of = jnp.zeros_like(plate_row)
    for k in range(plates):
        slot_of = jnp.where(plate_row == k, owner_ref[k], slot_of)
    body_at = jnp.where(live, slot_of * pb + rank[...], plates * pb)
    lane = lax.broadcasted_iota(jnp.int32, (1, TILE), 1)
    for t in range(tiles):
        info = jnp.where(lane == pairs, count_ref[t], 0)
        for s in range(pairs):
            info = jnp.where(lane == s, list_ref[t, s], info)
        ids[m * tiles + t] = jnp.concatenate([body_at[:, t * TILE : (t + 1) * TILE], info], axis=0)

    def ids_copy(e):
        here = ids.at[pl.ds(m * tiles, tiles)]
        return move(here, here, local_sem.at[2], data_sem.at[3], (r, e))

    for e in others:
        ids_copy(e).start()

    @pl.when(jnp.logical_not(has_low))
    def _():
        ext[pl.ds(0, half * tiles)] = jnp.zeros((half * tiles, ROWS, TILE), jnp.float32)

    @pl.when(jnp.logical_not(has_high))
    def _():
        ext[pl.ds((half + n_member) * tiles, half * tiles)] = jnp.zeros(
            (half * tiles, ROWS, TILE), jnp.float32
        )

    across = lax.broadcasted_iota(jnp.int32, (ROWS, TILE), 0) < 2
    middle = jnp.where(across, jnp.broadcast_to(packed[:, :1], (ROWS, TILE)), 0.0)
    last = ext.shape[0] - 1
    ext[last] = jnp.zeros((ROWS, TILE), jnp.float32)
    sources[last] = source_table(jnp.zeros((ROWS, TILE), jnp.float32), middle)

    def tabulate(first, count):
        @pl.loop(0, count)
        def _(i):
            for t in range(tiles):
                at = first + i * tiles + t
                sources[at] = source_table(ext[at], middle)

    tabulate(base, 1)
    for t in range(tiles):
        own = place_row[:, t * TILE : (t + 1) * TILE]
        for c in range(3):
            tgt[t * 3 + c] = jnp.broadcast_to(own[c : c + 1], (TILE, TILE)).T
        targets[t] = target_table(own - middle[:3])

    def some_pairs(t, tile_ids, first):
        columns = jnp.concatenate([sources[e] for e in tile_ids], axis=1)
        planes = jnp.dot(targets[t], columns, preferred_element_type=jnp.float32)
        for side, e in enumerate(tile_ids):
            rows = ext[e]
            y1, y2, h, f1, f2, f3 = [jnp.broadcast_to(rows[c : c + 1], (SUB, TILE)) for c in range(6)]
            h2 = h + h
            for b in range(TILE // SUB):
                at = pl.ds(b * SUB, SUB)
                near, image, full, mirror = [
                    planes[(b * PLANES + p) * SUB :][:SUB, side * TILE : (side + 1) * TILE]
                    for p in range(PLANES)
                ]
                d1 = tgt[t * 3, at] - y1
                d2 = tgt[t * 3 + 1, at] - y2
                x3 = tgt[t * 3 + 2, at]
                d3 = x3 - h
                w = lax.rsqrt(near)
                p = lax.rsqrt(image)
                w3 = w * w * w
                p2 = p * p
                p3 = p2 * p
                cp3 = (h2 * x3) * p3
                alpha = (w + w3) - (p + cp3)
                gamma = cp3 * p2 * mirror
                both = full * (w3 - p3) + gamma
                terms = (f1 * alpha + d1 * both, f2 * alpha + d2 * both, f3 * alpha + d3 * both + h2 * gamma)
                for k in range(3):
                    if first:
                        acc[t * 3 + k, at] = terms[k]
                    else:
                        acc[t * 3 + k, at] = acc[t * 3 + k, at] + terms[k]

    @pl.loop(0, tiles)
    def _(t):
        some_pairs(t, [base + t], True)

    sized(block(0, n_member - 1), local_sem.at[0], data_sem.at[0]).wait_recv()

    for e in others:
        tabulate((half + e) * tiles, 1)

    @pl.when(has_low)
    def _():
        sized(block(0, half), local_sem.at[0], data_sem.at[1]).wait_recv()

    @pl.when(has_high)
    def _():
        sized(block(0, half), local_sem.at[0], data_sem.at[2]).wait_recv()

    tabulate(0, half)
    tabulate((half + n_member) * tiles, half)
    zeros = jnp.zeros((VROWS - 3, TILE), jnp.float32)

    def vel_copy(e):
        return move(vel.at[m], vel.at[m], local_sem.at[3], vel_sem.at[m], (r, e))

    blocks = []
    for t in range(tiles):
        for s in range(1, pairs, 2):
            chosen = [jnp.where(k < count_ref[t], list_ref[t, k], last) for k in range(s, min(s + 2, pairs))]
            some_pairs(t, chosen, False)
        blocks.append([jnp.sum(acc[t * 3 + c].T, axis=0, keepdims=True) for c in range(3)] + [zeros])
    rows = jnp.concatenate([jnp.concatenate(block, axis=0) for block in blocks], axis=1)
    vel[m] = rows
    for e in peers:
        vel_copy(e).start()
    vel_out[...] = rows[:3]

    count = 2 * n_member * tiles
    gather_table(ext, count, table)

    sized(ids.at[pl.ds(0, (n_member - 1) * tiles)], local_sem.at[2], data_sem.at[3]).wait_recv()
    first_id = m * (own_plates * pb)
    room = own_plates * pb
    far_ids = [ids[far * tiles + t] for t in range(tiles)]
    local = jnp.concatenate([v[:1] for v in far_ids], axis=0) - first_id
    mine = jnp.logical_and(local >= 0, local < room)
    counted = jnp.concatenate(
        [mine.astype(jnp.float32), jnp.zeros((2 * SUB - tiles, TILE), jnp.float32)], axis=0
    ).astype(jnp.bfloat16)
    up_to = lax.broadcasted_iota(jnp.int32, (TILE, TILE), 0) <= lax.broadcasted_iota(jnp.int32, (TILE, TILE), 1)
    order_in = jnp.dot(
        counted, jnp.where(up_to, 1.0, 0.0).astype(jnp.bfloat16), preferred_element_type=jnp.float32
    )
    seat = lax.broadcasted_iota(jnp.int32, (TILE, TILE), 0).astype(jnp.float32)
    row = lax.broadcasted_iota(jnp.int32, (ROWS, TILE), 0)
    before = jnp.full((1, 1), -1.0, jnp.float32)
    chosen, columns = [], []
    for t in range(tiles):
        at = jnp.where(mine[t : t + 1], order_in[t : t + 1] + before, -1.0)
        before = before + order_in[t : t + 1, TILE - 1 :]
        chosen.append(jnp.where(seat == at, 1.0, 0.0))
        id_hi, id_lo, _ = split3(local[t : t + 1].astype(jnp.float32))
        extra = jnp.where(row == 0, t + 1.0, jnp.where(row == 1, id_hi, jnp.where(row == 2, id_lo, 0.0)))
        columns.append(jnp.concatenate([*split3(ext[(half + far) * tiles + t]), extra], axis=0))
    picked = lax.dot_general(
        jnp.concatenate(columns, axis=1).astype(jnp.bfloat16),
        jnp.concatenate(chosen, axis=1).astype(jnp.bfloat16),
        (((1,), (1,)), ((), ())),
        preferred_element_type=jnp.float32,
    )
    label = picked[3 * ROWS : 3 * ROWS + 1]
    far_id = picked[3 * ROWS + 1 : 3 * ROWS + 2] + picked[3 * ROWS + 2 : 3 * ROWS + 3]
    info = jnp.concatenate([v[1:] for v in far_ids], axis=0).astype(jnp.float32)
    info = jnp.concatenate([info, jnp.zeros((TILE - tiles, TILE), jnp.float32)], axis=0).T
    of_tile = lax.broadcasted_iota(jnp.int32, (2 * SUB, TILE), 0).astype(jnp.float32) + 1.0
    lists = jnp.dot(
        info[: 2 * SUB, : 2 * SUB].astype(jnp.bfloat16),
        jnp.where(of_tile == label, 1.0, 0.0).astype(jnp.bfloat16),
        preferred_element_type=jnp.float32,
    )
    unused = jnp.logical_and(row == 2, label == 0.0)
    parts = [jnp.where(unused, 1.0, picked[:ROWS]), picked[ROWS : 2 * ROWS], picked[2 * ROWS : 3 * ROWS]]
    x3 = (parts[0] + parts[1] + parts[2])[2:3]

    far_vel = jnp.concatenate(gathered_pairs(table, count, lists, parts, x3, pairs) + [zeros], axis=0)

    width = hot.shape[1] // own_plates
    place = lax.broadcasted_iota(jnp.int32, (hot.shape[1], TILE), 0)
    place_f = place.astype(jnp.float32)

    @pl.loop(0, n_member - 1)
    def _(j):
        e = jnp.where(j == 0, m, peer(jnp.maximum(j - 1, 0)))
        for t in range(tiles):
            local = ids[e * tiles + t][:1] - first_id
            row = jnp.full_like(local, -1)
            for k in range(own_plates):
                inside = jnp.logical_and(local >= k * pb, local < (k + 1) * pb)
                row = jnp.where(inside, local + k * (width - pb), row)
            hot[j, :, t * TILE : (t + 1) * TILE] = jnp.where(place == row, 1.0, 0.0).astype(jnp.bfloat16)

    def placed(e, hot_at):
        return lax.dot_general(
            vel[e].astype(jnp.bfloat16), hot_at, (((1,), (1,)), ((), ())), preferred_element_type=jnp.float32
        )

    far_row = jnp.full((1, TILE), -1.0, jnp.float32)
    for k in range(own_plates):
        inside = jnp.logical_and(far_id >= k * pb, far_id < (k + 1) * pb)
        far_row = jnp.where(inside, far_id + float(k * (width - pb)), far_row)
    far_row = jnp.where(label == 0.0, -1.0, far_row)
    far_hot = jnp.where(place_f == far_row, 1.0, 0.0).astype(jnp.bfloat16)
    far_vel = jnp.where(label == 0.0, 0.0, far_vel)

    body_all = placed(m, hot[0]) + lax.dot_general(
        far_vel.astype(jnp.bfloat16), far_hot, (((1,), (1,)), ((), ())), preferred_element_type=jnp.float32
    )
    for j, e in enumerate(peers):
        sized(vel.at[e], local_sem.at[3], vel_sem.at[e]).wait_recv()
        body_all = body_all + placed(e, hot[j + 1])

    order = 3 * pb
    total = 2 * width
    bodies = []
    for k in range(own_plates):
        part = body_all[:, k * width : (k + 1) * width]
        part = jnp.concatenate([part, jnp.zeros((VROWS, total - width), jnp.float32)], axis=1)
        body = part[0:1]
        for c in range(1, 3):
            body = body + pltpu.roll(part, c * pb, 1)[c : c + 1]
        bodies.append(body[:, :order])
    body_out[...] = jnp.concatenate(bodies, axis=0).astype(jnp.bfloat16)

    sized(block(0, n_member - 1), local_sem.at[0], data_sem.at[0]).wait_send()
    sized(ids.at[pl.ds(0, (n_member - 1) * tiles)], local_sem.at[2], data_sem.at[3]).wait_send()
    sized(vel.at[pl.ds(0, n_member - 2)], local_sem.at[3], vel_sem.at[0]).wait_send()

    @pl.when(jnp.logical_or(to_high, to_low))
    def _():
        sized(block(0, n_member), local_sem.at[1], data_sem.at[1]).wait_send()


def finish(vel_ref, body_ref, vel_out, body_out):
    vel_out[...] = vel_ref[...]
    body_out[...] = body_ref[...]


def on_device(n_region, n_member, positions, forces, blob_platelet, blob_rank, owner, pair_list, pair_count, pre):
    blobs = positions.shape[1]
    tiles = blobs // TILE
    own_plates, order, _ = pre.shape
    pb = order // 3
    width = -(-pb // TILE) * TILE
    depth = -(-3 * (2 * n_member * tiles + ROWS) // TILE) * TILE
    far = pl.BlockSpec(memory_space=pltpu.HBM)
    vector = pl.BlockSpec(memory_space=pltpu.VMEM)
    velocity, body_in = pl.pallas_call(
        functools.partial(kernel, n_region, n_member, pb, own_plates),
        out_shape=(
            pltpu.VMEM((3, blobs), jnp.float32),
            pltpu.VMEM((own_plates, order), jnp.bfloat16),
        ),
        in_specs=[far] * 7,
        out_specs=(vector, vector),
        scratch_shapes=[
            pltpu.VMEM((3, blobs), jnp.float32),
            pltpu.VMEM((3, blobs), jnp.float32),
            pltpu.VMEM((1, blobs), jnp.int32),
            pltpu.VMEM((1, blobs), jnp.int32),
            pltpu.SMEM(owner.shape, jnp.int32),
            pltpu.SMEM(pair_list.shape, jnp.int32),
            pltpu.SMEM(pair_count.shape, jnp.int32),
            pltpu.VMEM((2 * n_member * tiles + 1, ROWS, TILE), jnp.float32),
            pltpu.VMEM((n_member * tiles, 2, TILE), jnp.int32),
            pltpu.VMEM((2 * n_member * tiles + 1, DEPTH, TILE), jnp.bfloat16),
            pltpu.VMEM((tiles, PLANES * TILE, DEPTH), jnp.bfloat16),
            pltpu.VMEM((3 * tiles, TILE, TILE), jnp.float32),
            pltpu.VMEM((3 * tiles, TILE, TILE), jnp.float32),
            pltpu.VMEM((GATHER * TILE, depth), jnp.bfloat16),
            pltpu.VMEM((n_member, VROWS, blobs), jnp.float32),
            pltpu.VMEM((n_member - 1, own_plates * width, blobs), jnp.bfloat16),
            pltpu.SemaphoreType.DMA((7,)),
            pltpu.SemaphoreType.DMA((4,)),
            pltpu.SemaphoreType.DMA((n_member,)),
        ],
        compiler_params=pltpu.CompilerParams(collective_id=0, has_side_effects=True),
    )(
        positions,
        forces,
        blob_platelet,
        blob_rank,
        owner,
        pair_list,
        pair_count,
    )
    body_velocity = jnp.einsum("pab,pb->pa", pre, body_in, preferred_element_type=jnp.float32)
    return pl.pallas_call(
        finish,
        out_shape=(
            jax.ShapeDtypeStruct(velocity.shape, jnp.float32),
            jax.ShapeDtypeStruct(body_velocity.shape, jnp.float32),
        ),
        in_specs=[vector, vector],
        out_specs=(vector, vector),
        compiler_params=pltpu.CompilerParams(vmem_limit_bytes=1024 * 1024),
    )(velocity, body_velocity)


def solution(mesh):
    placed = (
        P(None, ("region", "member")),
        P(None, ("region", "member")),
        P(("region", "member")),
        P(("region", "member")),
        P("region"),
        P(("region", "member"), None),
        P(("region", "member")),
        P(("region", "member"), None, None),
    )
    return jax.shard_map(
        functools.partial(on_device, mesh.shape["region"], mesh.shape["member"]),
        mesh=mesh,
        in_specs=placed,
        out_specs=(P(None, ("region", "member")), P(("region", "member"), None)),
        check_vma=False,
    )
```

time: 15 us -> 13.8 us (0.920)
  Pallas kernels: 13.8 us -> 12.6 us
    pallas_call x1, Pallas kernels: 13.2 us -> 12 us  [on_device(): pl.pallas_call(functools.partial(kernel, n_region, n_member, pb, own_plat...]
where the time goes in v2:
time: 13.8 us; the launch traced here: 13.6 us
  Pallas kernels  12.6 us (91%)
  between operations  0.66 us (5%)
  matrix products  0.36 us (3%)
    pallas_call x1, Pallas kernels, on_device(): pl.pallas_call(functools.partial(kernel, n_region, n_member, pb, own_plat...  12 us
    pallas_call x1, Pallas kernels, on_device(): pl.pallas_call(finish, out_shape=(jax.ShapeDtypeStruct(velocity.shape, jn...  0.62 us
    dot_general x1, matrix products, on_device(): jnp.einsum('pab,pb->pa', pre, body_in, preferred_element_type=jnp.float32)  0.36 us

profile of v2, /device:TPU:0, one launch (start us, length us, event | category | flops | bytes accessed | tf_op | source)
XLA Modules:
  0.0 13.6 jit_solution(4162490496937063214)
XLA Ops:
  0.6 0.0 copy-start
  0.6 12.0 %shard_map.95 = (f32[3,384]{1,0:T(4,128)S(1)}, bf16[2,486]{1,0:T(2,128)(2,1)S(1)}) custom-call(f32[3,384]{1,0:T(4,128)} %pos_hbm.1, f32[3,384]{1,0:T(4,128)} %force_hbm.1, s32[384]{0:T(512)} %plate_hbm.1, s32[384]{0:T(512)} %rank_hbm.1, s32[8]{0:T(128)} %owner_hbm.1, s32[3,8]{1,0:T(4,128)} %list_hbm.1, s32[3]{0:T(128)} %count_hbm.1), custom_call_target="tpu_custom_call" | custom-call | tf_op jit(solution)/shard_map/pallas_call | solution.py:493
  12.6 0.0 copy-done
  12.6 0.4 %fusion = f32[2,1,486]{2,1,0:T(1,128)S(1)} fusion(bf16[2,486,486]{2,0,1:T(2,128)(2,1)S(1)} %copy-done, bf16[2,486,1]{1,0,2:T(2,128)(2,1)S(1)} %bitcast.5), kind=kOutput, calls=%fused_computation | convolution fusion | flops 944784 | bytes 950616 | tf_op jit(solution)/shard_map/pab,pb->pa/dot_general | solution.py:532
  13.0 0.6 %shard_map.96 = (f32[3,384]{1,0:T(4,128)}, f32[2,486]{1,0:T(2,128)}) custom-call(f32[3,384]{1,0:T(4,128)S(1)} %get-tuple-element.4.vel_ref, f32[2,486]{1,0:T(2,128)S(1)} %bitcast.4), custom_call_target="tpu_custom_call" | custom-call | tf_op jit(solution)/shard_map/pallas_call | solution.py:533
  (1 shorter events, 0.0 us)
Async XLA Ops:
  0.6 12.0 %copy-start = (bf16[2,486,486]{2,0,1:T(2,128)(2,1)S(1)}, bf16[2,486,486]{2,0,1:T(2,128)(2,1)}, u32[]{:S(2)}) copy-start(bf16[2,486,486]{2,0,1:T(2,128)(2,1)} %param.15) | copy-start | bytes 2834356

commit v3 on v2

--- a/solution.py
+++ b/solution.py
@@ -144,7 +144,6 @@
     list_ref,
     count_ref,
     ext,
-    ids,
     sources,
     targets,
     tgt,
@@ -177,7 +176,7 @@
         return jnp.where(j % 2 == 0, mate, n_member - 1 - mate)
 
     peers = [peer(j) for j in range(n_member - 2)]
-    others = peers + [far]
+    others = [far] + peers
 
     barrier = pltpu.get_barrier_semaphore()
     for e in others:
@@ -206,15 +205,26 @@
     for load in loads[3:]:
         load.start()
 
-    for load in loads[:3]:
+    for load in loads:
         load.wait()
 
     live = plate[...] < plates
     place_row = pos[...]
     push_row = force[...] * jnp.where(live, SCALE, 0.0)
-    packed = jnp.concatenate([place_row, push_row, jnp.zeros((ROWS - 6, blobs), jnp.float32)], axis=0)
+    plate_row = plate[...]
+    slot_of = jnp.zeros_like(plate_row)
+    for k in range(plates):
+        slot_of = jnp.where(plate_row == k, owner_ref[k], slot_of)
+    body_at = jnp.where(live, slot_of * pb + rank[...], plates * pb).astype(jnp.float32)
+    lane = lax.broadcasted_iota(jnp.int32, (1, TILE), 1)
     for t in range(tiles):
-        ext[base + t] = packed[:, t * TILE : (t + 1) * TILE]
+        span = slice(t * TILE, (t + 1) * TILE)
+        info = jnp.where(lane == pairs, count_ref[t], 0)
+        for s in range(pairs):
+            info = jnp.where(lane == s, list_ref[t, s], info)
+        ext[base + t] = jnp.concatenate(
+            [place_row[:, span], push_row[:, span], body_at[:, span], info.astype(jnp.float32)], axis=0
+        )
 
     def block(e, count=1):
         return ext.at[pl.ds(e * tiles, count * tiles)]
@@ -250,28 +260,6 @@
         for k in range(n_member):
             rim_copy(k, -1, half + n_member + m, 2).start()
 
-    for load in loads[3:]:
-        load.wait()
-
-    plate_row = plate[...]
-    slot_of = jnp.zeros_like(plate_row)
-    for k in range(plates):
-        slot_of = jnp.where(plate_row == k, owner_ref[k], slot_of)
-    body_at = jnp.where(live, slot_of * pb + rank[...], plates * pb)
-    lane = lax.broadcasted_iota(jnp.int32, (1, TILE), 1)
-    for t in range(tiles):
-        info = jnp.where(lane == pairs, count_ref[t], 0)
-        for s in range(pairs):
-            info = jnp.where(lane == s, list_ref[t, s], info)
-        ids[m * tiles + t] = jnp.concatenate([body_at[:, t * TILE : (t + 1) * TILE], info], axis=0)
-
-    def ids_copy(e):
-        here = ids.at[pl.ds(m * tiles, tiles)]
-        return move(here, here, local_sem.at[2], data_sem.at[3], (r, e))
-
-    for e in others:
-        ids_copy(e).start()
-
     @pl.when(jnp.logical_not(has_low))
     def _():
         ext[pl.ds(0, half * tiles)] = jnp.zeros((half * tiles, ROWS, TILE), jnp.float32)
@@ -283,7 +271,7 @@
         )
 
     across = lax.broadcasted_iota(jnp.int32, (ROWS, TILE), 0) < 2
-    middle = jnp.where(across, jnp.broadcast_to(packed[:, :1], (ROWS, TILE)), 0.0)
+    middle = jnp.where(across, jnp.broadcast_to(ext[base][:, :1], (ROWS, TILE)), 0.0)
     last = ext.shape[0] - 1
     ext[last] = jnp.zeros((ROWS, TILE), jnp.float32)
     sources[last] = source_table(jnp.zeros((ROWS, TILE), jnp.float32), middle)
@@ -374,12 +362,11 @@
     count = 2 * n_member * tiles
     gather_table(ext, count, table)
 
-    sized(ids.at[pl.ds(0, (n_member - 1) * tiles)], local_sem.at[2], data_sem.at[3]).wait_recv()
-    first_id = m * (own_plates * pb)
+    first_id = (m * (own_plates * pb)).astype(jnp.float32)
     room = own_plates * pb
-    far_ids = [ids[far * tiles + t] for t in range(tiles)]
-    local = jnp.concatenate([v[:1] for v in far_ids], axis=0) - first_id
-    mine = jnp.logical_and(local >= 0, local < room)
+    far_tiles = [ext[(half + far) * tiles + t] for t in range(tiles)]
+    local = jnp.concatenate([v[6:7] for v in far_tiles], axis=0) - first_id
+    mine = jnp.logical_and(local >= 0.0, local < float(room))
     counted = jnp.concatenate(
         [mine.astype(jnp.float32), jnp.zeros((2 * SUB - tiles, TILE), jnp.float32)], axis=0
     ).astype(jnp.bfloat16)
@@ -395,9 +382,9 @@
         at = jnp.where(mine[t : t + 1], order_in[t : t + 1] + before, -1.0)
         before = before + order_in[t : t + 1, TILE - 1 :]
         chosen.append(jnp.where(seat == at, 1.0, 0.0))
-        id_hi, id_lo, _ = split3(local[t : t + 1].astype(jnp.float32))
+        id_hi, id_lo, _ = split3(jnp.where(mine[t : t + 1], local[t : t + 1], 0.0))
         extra = jnp.where(row == 0, t + 1.0, jnp.where(row == 1, id_hi, jnp.where(row == 2, id_lo, 0.0)))
-        columns.append(jnp.concatenate([*split3(ext[(half + far) * tiles + t]), extra], axis=0))
+        columns.append(jnp.concatenate([*split3(far_tiles[t]), extra], axis=0))
     picked = lax.dot_general(
         jnp.concatenate(columns, axis=1).astype(jnp.bfloat16),
         jnp.concatenate(chosen, axis=1).astype(jnp.bfloat16),
@@ -406,7 +393,7 @@
     )
     label = picked[3 * ROWS : 3 * ROWS + 1]
     far_id = picked[3 * ROWS + 1 : 3 * ROWS + 2] + picked[3 * ROWS + 2 : 3 * ROWS + 3]
-    info = jnp.concatenate([v[1:] for v in far_ids], axis=0).astype(jnp.float32)
+    info = jnp.concatenate([v[7:8] for v in far_tiles], axis=0)
     info = jnp.concatenate([info, jnp.zeros((TILE - tiles, TILE), jnp.float32)], axis=0).T
     of_tile = lax.broadcasted_iota(jnp.int32, (2 * SUB, TILE), 0).astype(jnp.float32) + 1.0
     lists = jnp.dot(
@@ -420,55 +407,75 @@
 
     far_vel = jnp.concatenate(gathered_pairs(table, count, lists, parts, x3, pairs) + [zeros], axis=0)
 
-    width = hot.shape[1] // own_plates
-    place = lax.broadcasted_iota(jnp.int32, (hot.shape[1], TILE), 0)
-    place_f = place.astype(jnp.float32)
-
-    @pl.loop(0, n_member - 1)
-    def _(j):
-        e = jnp.where(j == 0, m, peer(jnp.maximum(j - 1, 0)))
+    place = lax.broadcasted_iota(jnp.int32, (hot.shape[1], TILE), 0).astype(jnp.float32)
+
+    def seats(at):
+        return jnp.where(place == at, 1.0, 0.0).astype(jnp.bfloat16)
+
+    for j, e in enumerate([m] + peers):
         for t in range(tiles):
-            local = ids[e * tiles + t][:1] - first_id
-            row = jnp.full_like(local, -1)
-            for k in range(own_plates):
-                inside = jnp.logical_and(local >= k * pb, local < (k + 1) * pb)
-                row = jnp.where(inside, local + k * (width - pb), row)
-            hot[j, :, t * TILE : (t + 1) * TILE] = jnp.where(place == row, 1.0, 0.0).astype(jnp.bfloat16)
-
-    def placed(e, hot_at):
-        return lax.dot_general(
-            vel[e].astype(jnp.bfloat16), hot_at, (((1,), (1,)), ((), ())), preferred_element_type=jnp.float32
+            hot[j, :, t * TILE : (t + 1) * TILE] = seats(ext[(half + e) * tiles + t][6:7] - first_id)
+
+    slots = [m] + peers
+    row = lax.broadcasted_iota(jnp.int32, (ROWS, TILE), 0)
+    slot_lane = lax.broadcasted_iota(jnp.int32, (ROWS, TILE), 1).astype(jnp.float32)
+    source = jnp.zeros((ROWS, hot.shape[1]), jnp.float32)
+    for j in range(len(slots)):
+        names = [jnp.where(row == 0, slot_lane, j * tiles + t + 1.0) for t in range(tiles)]
+        source = source + lax.dot_general(
+            jnp.concatenate(names, axis=1).astype(jnp.bfloat16),
+            hot[j],
+            (((1,), (1,)), ((), ())),
+            preferred_element_type=jnp.float32,
         )
-
-    far_row = jnp.full((1, TILE), -1.0, jnp.float32)
-    for k in range(own_plates):
-        inside = jnp.logical_and(far_id >= k * pb, far_id < (k + 1) * pb)
-        far_row = jnp.where(inside, far_id + float(k * (width - pb)), far_row)
-    far_row = jnp.where(label == 0.0, -1.0, far_row)
-    far_hot = jnp.where(place_f == far_row, 1.0, 0.0).astype(jnp.bfloat16)
-    far_vel = jnp.where(label == 0.0, 0.0, far_vel)
-
-    body_all = placed(m, hot[0]) + lax.dot_general(
-        far_vel.astype(jnp.bfloat16), far_hot, (((1,), (1,)), ((), ())), preferred_element_type=jnp.float32
-    )
-    for j, e in enumerate(peers):
+    body_all = lax.dot_general(
+        jnp.where(label == 0.0, 0.0, far_vel).astype(jnp.bfloat16),
+        seats(jnp.where(label == 0.0, -1.0, far_id)),
+        (((1,), (1,)), ((), ())),
+        preferred_element_type=jnp.float32,
+    )
+    spans = [slice(k, k + TILE) for k in range(0, hot.shape[1], TILE)]
+    from_lane = [jnp.broadcast_to(source[:1, span].astype(jnp.int32), (ROWS, TILE)) for span in spans]
+    from_name = [jnp.broadcast_to(source[1:2, span], (ROWS, TILE)) for span in spans]
+    body_all = jnp.concatenate([body_all, jnp.zeros((ROWS - VROWS, hot.shape[1]), jnp.float32)], axis=0)
+    seated = [body_all[:, span] for span in spans]
+
+    def seat(j, seated):
+        values = vel[slots[j]]
+        values = jnp.concatenate([values, jnp.zeros((ROWS - VROWS, blobs), jnp.float32)], axis=0)
+        for t in range(tiles):
+            tile = values[:, t * TILE : (t + 1) * TILE]
+            seated = [
+                jnp.where(name == j * tiles + t + 1.0, jnp.take_along_axis(tile, at, axis=1), old)
+                for name, at, old in zip(from_name, from_lane, seated)
+            ]
+        return seated
+
+    seated = seat(0, seated)
+
+    for e in peers:
         sized(vel.at[e], local_sem.at[3], vel_sem.at[e]).wait_recv()
-        body_all = body_all + placed(e, hot[j + 1])
-
+
+    for j in range(1, len(slots)):
+        seated = seat(j, seated)
+    body_all = jnp.concatenate(seated, axis=1)[:VROWS]
     order = 3 * pb
-    total = 2 * width
+    total = -(-order // TILE) * TILE
+    body_all = jnp.concatenate([body_all, jnp.zeros((VROWS, total - hot.shape[1]), jnp.float32)], axis=1)
+    lane = lax.broadcasted_iota(jnp.int32, (VROWS, total), 1)
+    parts = [
+        jnp.where(jnp.logical_and(lane >= k * pb, lane < (k + 1) * pb), body_all, 0.0) for k in range(own_plates)
+    ]
     bodies = []
     for k in range(own_plates):
-        part = body_all[:, k * width : (k + 1) * width]
-        part = jnp.concatenate([part, jnp.zeros((VROWS, total - width), jnp.float32)], axis=1)
-        body = part[0:1]
-        for c in range(1, 3):
-            body = body + pltpu.roll(part, c * pb, 1)[c : c + 1]
+        body = jnp.zeros((1, total), jnp.float32)
+        for c in range(3):
+            shift = (c - k) * pb % total
+            body = body + (pltpu.roll(parts[k], shift, 1) if shift else parts[k])[c : c + 1]
         bodies.append(body[:, :order])
     body_out[...] = jnp.concatenate(bodies, axis=0).astype(jnp.bfloat16)
 
     sized(block(0, n_member - 1), local_sem.at[0], data_sem.at[0]).wait_send()
-    sized(ids.at[pl.ds(0, (n_member - 1) * tiles)], local_sem.at[2], data_sem.at[3]).wait_send()
     sized(vel.at[pl.ds(0, n_member - 2)], local_sem.at[3], vel_sem.at[0]).wait_send()
 
     @pl.when(jnp.logical_or(to_high, to_low))
@@ -486,7 +493,7 @@
     tiles = blobs // TILE
     own_plates, order, _ = pre.shape
     pb = order // 3
-    width = -(-pb // TILE) * TILE
+    seats = -(-own_plates * pb // TILE) * TILE
     depth = -(-3 * (2 * n_member * tiles + ROWS) // TILE) * TILE
     far = pl.BlockSpec(memory_space=pltpu.HBM)
     vector = pl.BlockSpec(memory_space=pltpu.VMEM)
@@ -507,16 +514,15 @@
             pltpu.SMEM(pair_list.shape, jnp.int32),
             pltpu.SMEM(pair_count.shape, jnp.int32),
             pltpu.VMEM((2 * n_member * tiles + 1, ROWS, TILE), jnp.float32),
-            pltpu.VMEM((n_member * tiles, 2, TILE), jnp.int32),
             pltpu.VMEM((2 * n_member * tiles + 1, DEPTH, TILE), jnp.bfloat16),
             pltpu.VMEM((tiles, PLANES * TILE, DEPTH), jnp.bfloat16),
             pltpu.VMEM((3 * tiles, TILE, TILE), jnp.float32),
             pltpu.VMEM((3 * tiles, TILE, TILE), jnp.float32),
             pltpu.VMEM((GATHER * TILE, depth), jnp.bfloat16),
             pltpu.VMEM((n_member, VROWS, blobs), jnp.float32),
-            pltpu.VMEM((n_member - 1, own_plates * width, blobs), jnp.bfloat16),
+            pltpu.VMEM((n_member - 1, seats, blobs), jnp.bfloat16),
             pltpu.SemaphoreType.DMA((7,)),
-            pltpu.SemaphoreType.DMA((4,)),
+            pltpu.SemaphoreType.DMA((3,)),
             pltpu.SemaphoreType.DMA((n_member,)),
         ],
         compiler_params=pltpu.CompilerParams(collective_id=0, has_side_effects=True),

time: 13.8 us -> 13.5 us (0.978)
  Pallas kernels: 12.6 us -> 12.3 us
    pallas_call x1, Pallas kernels: 12 us -> 11.7 us  [on_device(): pl.pallas_call(functools.partial(kernel, n_region, n_member, pb, own_plat...]
where the time goes in v3:
time: 13.5 us; the launch traced here: 13.4 us
  Pallas kernels  12.3 us (91%)
  between operations  0.66 us (5%)
  matrix products  0.36 us (3%)
    pallas_call x1, Pallas kernels, on_device(): pl.pallas_call(functools.partial(kernel, n_region, n_member, pb, own_plat...  11.7 us
    pallas_call x1, Pallas kernels, on_device(): pl.pallas_call(finish, out_shape=(jax.ShapeDtypeStruct(velocity.shape, jn...  0.62 us
    dot_general x1, matrix products, on_device(): jnp.einsum('pab,pb->pa', pre, body_in, preferred_element_type=jnp.float32)  0.36 us

profile of v3, /device:TPU:0, one launch (start us, length us, event | category | flops | bytes accessed | tf_op | source)
XLA Modules:
  0.0 13.4 jit_solution(7124794903513132851)
XLA Ops:
  0.6 0.0 copy-start
  0.6 11.7 %shard_map.95 = (f32[3,384]{1,0:T(4,128)S(1)}, bf16[2,486]{1,0:T(2,128)(2,1)S(1)}) custom-call(f32[3,384]{1,0:T(4,128)} %pos_hbm.1, f32[3,384]{1,0:T(4,128)} %force_hbm.1, s32[384]{0:T(512)} %plate_hbm.1, s32[384]{0:T(512)} %rank_hbm.1, s32[8]{0:T(128)} %owner_hbm.1, s32[3,8]{1,0:T(4,128)} %list_hbm.1, s32[3]{0:T(128)} %count_hbm.1), custom_call_target="tpu_custom_call" | custom-call | tf_op jit(solution)/shard_map/pallas_call | solution.py:500
  12.4 0.0 copy-done
  12.4 0.4 %fusion = f32[2,1,486]{2,1,0:T(1,128)S(1)} fusion(bf16[2,486,486]{2,0,1:T(2,128)(2,1)S(1)} %copy-done, bf16[2,486,1]{1,0,2:T(2,128)(2,1)S(1)} %bitcast.5), kind=kOutput, calls=%fused_computation | convolution fusion | flops 944784 | bytes 950616 | tf_op jit(solution)/shard_map/pab,pb->pa/dot_general | solution.py:538
  12.7 0.6 %shard_map.96 = (f32[3,384]{1,0:T(4,128)}, f32[2,486]{1,0:T(2,128)}) custom-call(f32[3,384]{1,0:T(4,128)S(1)} %get-tuple-element.4.vel_ref, f32[2,486]{1,0:T(2,128)S(1)} %bitcast.4), custom_call_target="tpu_custom_call" | custom-call | tf_op jit(solution)/shard_map/pallas_call | solution.py:539
  (1 shorter events, 0.0 us)
Async XLA Ops:
  0.6 11.7 %copy-start = (bf16[2,486,486]{2,0,1:T(2,128)(2,1)S(1)}, bf16[2,486,486]{2,0,1:T(2,128)(2,1)}, u32[]{:S(2)}) copy-start(bf16[2,486,486]{2,0,1:T(2,128)(2,1)} %param.15) | copy-start | bytes 2834356

commit v4 on v3

--- a/solution.py
+++ b/solution.py
@@ -151,9 +151,9 @@
     table,
     vel,
     hot,
+    found,
     local_sem,
     data_sem,
-    vel_sem,
 ):
     r = lax.axis_index("region")
     m = lax.axis_index("member")
@@ -247,8 +247,8 @@
     rim_sends = jnp.where(jnp.logical_or(to_high, to_low), n_member, 0)
     pl.semaphore_wait(barrier, n_member - 1 + rim_sends)
 
-    for e in others:
-        near_copy(e).start()
+    for late, early in zip(peers + [far], [far] + peers):
+        near_copy(jnp.where(lower == 0, late, early)).start()
 
     @pl.when(to_high)
     def _():
@@ -327,25 +327,47 @@
     def _(t):
         some_pairs(t, [base + t], True)
 
+    first_id = (m * (own_plates * pb)).astype(jnp.float32)
+    place = lax.broadcasted_iota(jnp.int32, (hot.shape[1], TILE), 0).astype(jnp.float32)
+    slots = [m] + peers
+    name_row = lax.broadcasted_iota(jnp.int32, (ROWS, TILE), 0)
+    slot_lane = lax.broadcasted_iota(jnp.int32, (ROWS, TILE), 1).astype(jnp.float32)
+
+    def seats(at):
+        return jnp.where(place == at, 1.0, 0.0).astype(jnp.bfloat16)
+
+    def find(j):
+        for t in range(tiles):
+            hot[j, :, t * TILE : (t + 1) * TILE] = seats(ext[(half + slots[j]) * tiles + t][6:7] - first_id)
+        names = [jnp.where(name_row == 0, slot_lane, j * tiles + t + 1.0) for t in range(tiles)]
+        return lax.dot_general(
+            jnp.concatenate(names, axis=1).astype(jnp.bfloat16),
+            hot[j],
+            (((1,), (1,)), ((), ())),
+            preferred_element_type=jnp.float32,
+        )
+
+    found[...] = find(0)
+
+    @pl.when(has_low)
+    def _():
+        sized(block(0, half), local_sem.at[0], data_sem.at[1]).wait_recv()
+
+    @pl.when(has_high)
+    def _():
+        sized(block(0, half), local_sem.at[0], data_sem.at[2]).wait_recv()
+
+    tabulate(0, half)
+    tabulate((half + n_member) * tiles, half)
     sized(block(0, n_member - 1), local_sem.at[0], data_sem.at[0]).wait_recv()
 
     for e in others:
         tabulate((half + e) * tiles, 1)
 
-    @pl.when(has_low)
-    def _():
-        sized(block(0, half), local_sem.at[0], data_sem.at[1]).wait_recv()
-
-    @pl.when(has_high)
-    def _():
-        sized(block(0, half), local_sem.at[0], data_sem.at[2]).wait_recv()
-
-    tabulate(0, half)
-    tabulate((half + n_member) * tiles, half)
     zeros = jnp.zeros((VROWS - 3, TILE), jnp.float32)
 
     def vel_copy(e):
-        return move(vel.at[m], vel.at[m], local_sem.at[3], vel_sem.at[m], (r, e))
+        return move(vel.at[m], vel.at[m], local_sem.at[3], data_sem.at[3], (r, e))
 
     blocks = []
     for t in range(tiles):
@@ -362,7 +384,6 @@
     count = 2 * n_member * tiles
     gather_table(ext, count, table)
 
-    first_id = (m * (own_plates * pb)).astype(jnp.float32)
     room = own_plates * pb
     far_tiles = [ext[(half + far) * tiles + t] for t in range(tiles)]
     local = jnp.concatenate([v[6:7] for v in far_tiles], axis=0) - first_id
@@ -407,76 +428,63 @@
 
     far_vel = jnp.concatenate(gathered_pairs(table, count, lists, parts, x3, pairs) + [zeros], axis=0)
 
-    place = lax.broadcasted_iota(jnp.int32, (hot.shape[1], TILE), 0).astype(jnp.float32)
-
-    def seats(at):
-        return jnp.where(place == at, 1.0, 0.0).astype(jnp.bfloat16)
-
-    for j, e in enumerate([m] + peers):
-        for t in range(tiles):
-            hot[j, :, t * TILE : (t + 1) * TILE] = seats(ext[(half + e) * tiles + t][6:7] - first_id)
-
-    slots = [m] + peers
-    row = lax.broadcasted_iota(jnp.int32, (ROWS, TILE), 0)
-    slot_lane = lax.broadcasted_iota(jnp.int32, (ROWS, TILE), 1).astype(jnp.float32)
-    source = jnp.zeros((ROWS, hot.shape[1]), jnp.float32)
-    for j in range(len(slots)):
-        names = [jnp.where(row == 0, slot_lane, j * tiles + t + 1.0) for t in range(tiles)]
-        source = source + lax.dot_general(
-            jnp.concatenate(names, axis=1).astype(jnp.bfloat16),
-            hot[j],
-            (((1,), (1,)), ((), ())),
-            preferred_element_type=jnp.float32,
-        )
+    order = 3 * pb
+    total = -(-order // TILE) * TILE
+    source = found[...]
+    for j in range(1, len(slots)):
+        source = source + find(j)
+
+    def spread(v, k, fill):
+        v = jnp.concatenate([v, jnp.zeros((v.shape[0], total - v.shape[1]), jnp.float32)], axis=1)
+        lane = lax.broadcasted_iota(jnp.int32, v.shape, 1)
+        v = jnp.where(jnp.logical_and(lane >= k * pb, lane < (k + 1) * pb), v, fill)
+        shifts = [(c - k) * pb % total for c in range(3)]
+        return [pltpu.roll(v, shift, 1) if shift else v for shift in shifts]
+
     body_all = lax.dot_general(
         jnp.where(label == 0.0, 0.0, far_vel).astype(jnp.bfloat16),
         seats(jnp.where(label == 0.0, -1.0, far_id)),
         (((1,), (1,)), ((), ())),
         preferred_element_type=jnp.float32,
     )
-    spans = [slice(k, k + TILE) for k in range(0, hot.shape[1], TILE)]
-    from_lane = [jnp.broadcast_to(source[:1, span].astype(jnp.int32), (ROWS, TILE)) for span in spans]
-    from_name = [jnp.broadcast_to(source[1:2, span], (ROWS, TILE)) for span in spans]
-    body_all = jnp.concatenate([body_all, jnp.zeros((ROWS - VROWS, hot.shape[1]), jnp.float32)], axis=0)
-    seated = [body_all[:, span] for span in spans]
-
-    def seat(j, seated):
-        values = vel[slots[j]]
-        values = jnp.concatenate([values, jnp.zeros((ROWS - VROWS, blobs), jnp.float32)], axis=0)
+    part_of = lax.broadcasted_iota(jnp.int32, (1, total), 1)
+    part_of = [part_of < (c + 1) * pb for c in range(3)]
+    spans = [slice(k, k + TILE) for k in range(0, total, TILE)]
+    from_lane, from_name, body = [], [], []
+    for k in range(own_plates):
+        table_k = spread(source, k, 0.0)
+        table_k = table_k[0] + table_k[1] + table_k[2]
+        from_lane += [jnp.broadcast_to(table_k[:1, v].astype(jnp.int32), (ROWS, TILE)) for v in spans]
+        from_name += [jnp.broadcast_to(table_k[1:2, v], (ROWS, TILE)) for v in spans]
+        fixed = spread(body_all, k, 0.0)
+        fixed = fixed[0][0:1] + fixed[1][1:2] + fixed[2][2:3]
+        body += [jnp.broadcast_to(fixed[:, v], (ROWS, TILE)) for v in spans]
+
+    def seat(j, body):
+        values = jnp.concatenate([vel[slots[j]], jnp.zeros((ROWS - VROWS, blobs), jnp.float32)], axis=0)
         for t in range(tiles):
             tile = values[:, t * TILE : (t + 1) * TILE]
-            seated = [
+            body = [
                 jnp.where(name == j * tiles + t + 1.0, jnp.take_along_axis(tile, at, axis=1), old)
-                for name, at, old in zip(from_name, from_lane, seated)
+                for name, at, old in zip(from_name, from_lane, body)
             ]
-        return seated
-
-    seated = seat(0, seated)
-
-    for e in peers:
-        sized(vel.at[e], local_sem.at[3], vel_sem.at[e]).wait_recv()
+        return body
+
+    body = seat(0, body)
+
+    sized(vel.at[pl.ds(0, n_member - 2)], local_sem.at[3], data_sem.at[3]).wait_recv()
 
     for j in range(1, len(slots)):
-        seated = seat(j, seated)
-    body_all = jnp.concatenate(seated, axis=1)[:VROWS]
-    order = 3 * pb
-    total = -(-order // TILE) * TILE
-    body_all = jnp.concatenate([body_all, jnp.zeros((VROWS, total - hot.shape[1]), jnp.float32)], axis=1)
-    lane = lax.broadcasted_iota(jnp.int32, (VROWS, total), 1)
-    parts = [
-        jnp.where(jnp.logical_and(lane >= k * pb, lane < (k + 1) * pb), body_all, 0.0) for k in range(own_plates)
-    ]
+        body = seat(j, body)
     bodies = []
     for k in range(own_plates):
-        body = jnp.zeros((1, total), jnp.float32)
-        for c in range(3):
-            shift = (c - k) * pb % total
-            body = body + (pltpu.roll(parts[k], shift, 1) if shift else parts[k])[c : c + 1]
-        bodies.append(body[:, :order])
+        rows = jnp.concatenate(body[k * len(spans) : (k + 1) * len(spans)], axis=1)
+        row = jnp.where(part_of[0], rows[0:1], jnp.where(part_of[1], rows[1:2], rows[2:3]))
+        bodies.append(row[:, :order])
     body_out[...] = jnp.concatenate(bodies, axis=0).astype(jnp.bfloat16)
 
     sized(block(0, n_member - 1), local_sem.at[0], data_sem.at[0]).wait_send()
-    sized(vel.at[pl.ds(0, n_member - 2)], local_sem.at[3], vel_sem.at[0]).wait_send()
+    sized(vel.at[pl.ds(0, n_member - 2)], local_sem.at[3], data_sem.at[3]).wait_send()
 
     @pl.when(jnp.logical_or(to_high, to_low))
     def _():
@@ -521,9 +529,9 @@
             pltpu.VMEM((GATHER * TILE, depth), jnp.bfloat16),
             pltpu.VMEM((n_member, VROWS, blobs), jnp.float32),
             pltpu.VMEM((n_member - 1, seats, blobs), jnp.bfloat16),
+            pltpu.VMEM((ROWS, seats), jnp.float32),
             pltpu.SemaphoreType.DMA((7,)),
-            pltpu.SemaphoreType.DMA((3,)),
-            pltpu.SemaphoreType.DMA((n_member,)),
+            pltpu.SemaphoreType.DMA((4,)),
         ],
         compiler_params=pltpu.CompilerParams(collective_id=0, has_side_effects=True),
     )(

time: 13.5 us -> 13.3 us (0.985)
    pallas_call x1, Pallas kernels: 11.7 us -> 11.5 us  [on_device(): pl.pallas_call(functools.partial(kernel, n_region, n_member, pb, own_plat...]
where the time goes in v4:
time: 13.3 us; the launch traced here: 13.2 us
  Pallas kernels  12.2 us (92%)
  between operations  0.66 us (5%)
  matrix products  0.36 us (3%)
    pallas_call x1, Pallas kernels, on_device(): pl.pallas_call(functools.partial(kernel, n_region, n_member, pb, own_plat...  11.5 us
    pallas_call x1, Pallas kernels, on_device(): pl.pallas_call(finish, out_shape=(jax.ShapeDtypeStruct(velocity.shape, jn...  0.62 us
    dot_general x1, matrix products, on_device(): jnp.einsum('pab,pb->pa', pre, body_in, preferred_element_type=jnp.float32)  0.36 us

profile of v4, /device:TPU:0, one launch (start us, length us, event | category | flops | bytes accessed | tf_op | source)
XLA Modules:
  0.0 13.2 jit_solution(15853754614635798191)
XLA Ops:
  0.6 0.0 copy-start
  0.6 11.5 %shard_map.95 = (f32[3,384]{1,0:T(4,128)S(1)}, bf16[2,486]{1,0:T(2,128)(2,1)S(1)}) custom-call(f32[3,384]{1,0:T(4,128)} %pos_hbm.1, f32[3,384]{1,0:T(4,128)} %force_hbm.1, s32[384]{0:T(512)} %plate_hbm.1, s32[384]{0:T(512)} %rank_hbm.1, s32[8]{0:T(128)} %owner_hbm.1, s32[3,8]{1,0:T(4,128)} %list_hbm.1, s32[3]{0:T(128)} %count_hbm.1), custom_call_target="tpu_custom_call" | custom-call | tf_op jit(solution)/shard_map/pallas_call | solution.py:508
  12.2 0.0 copy-done
  12.2 0.4 %fusion = f32[2,1,486]{2,1,0:T(1,128)S(1)} fusion(bf16[2,486,486]{2,0,1:T(2,128)(2,1)S(1)} %copy-done, bf16[2,486,1]{1,0,2:T(2,128)(2,1)S(1)} %bitcast.5), kind=kOutput, calls=%fused_computation | convolution fusion | flops 944784 | bytes 950616 | tf_op jit(solution)/shard_map/pab,pb->pa/dot_general | solution.py:546
  12.6 0.6 %shard_map.96 = (f32[3,384]{1,0:T(4,128)}, f32[2,486]{1,0:T(2,128)}) custom-call(f32[3,384]{1,0:T(4,128)S(1)} %get-tuple-element.4.vel_ref, f32[2,486]{1,0:T(2,128)S(1)} %bitcast.4), custom_call_target="tpu_custom_call" | custom-call | tf_op jit(solution)/shard_map/pallas_call | solution.py:547
  (1 shorter events, 0.0 us)
Async XLA Ops:
  0.6 11.6 %copy-start = (bf16[2,486,486]{2,0,1:T(2,128)(2,1)S(1)}, bf16[2,486,486]{2,0,1:T(2,128)(2,1)}, u32[]{:S(2)}) copy-start(bf16[2,486,486]{2,0,1:T(2,128)(2,1)} %param.15) | copy-start | bytes 2834356

commit v5 on v4

--- a/solution.py
+++ b/solution.py
@@ -12,7 +12,7 @@
 SUB = 8
 VROWS = 4
 ROWS = 8
-PLANES = 4
+PLANES = 5
 DEPTH = 64
 GATHER = 7
 SCALE = 1.0 / (8.0 * math.pi)
@@ -47,6 +47,7 @@
     planes = [
         plane([-2.0 * x1, -2.0 * x2, -2.0 * x3] + none, squares + 1.0, (one, zero)),
         plane([-2.0 * x1, -2.0 * x2, 2.0 * x3] + none, squares, (one, zero)),
+        plane([zero, zero, 2.0 * x3] + none),
         plane(none + [x1, x2, x3], (), (zero, -one)),
         plane(none + [3.0 * x1, 3.0 * x2, -3.0 * x3], (), (zero, -3.0 * one)),
     ]
@@ -154,6 +155,7 @@
     found,
     local_sem,
     data_sem,
+    far_ready,
 ):
     r = lax.axis_index("region")
     m = lax.axis_index("member")
@@ -179,7 +181,13 @@
     others = [far] + peers
 
     barrier = pltpu.get_barrier_semaphore()
-    for e in others:
+    first_end, last_end = m == 0, m == n_member - 1
+
+    @pl.when(jnp.logical_not(last_end))
+    def _():
+        pl.semaphore_signal(barrier, inc=1, device_id=(r, far), device_id_type=MESH)
+
+    for e in peers:
         pl.semaphore_signal(barrier, inc=1, device_id=(r, e), device_id_type=MESH)
 
     loads = [
@@ -245,10 +253,19 @@
         return move(ref, ref, send, recv, (r, far))
 
     rim_sends = jnp.where(jnp.logical_or(to_high, to_low), n_member, 0)
-    pl.semaphore_wait(barrier, n_member - 1 + rim_sends)
-
-    for late, early in zip(peers + [far], [far] + peers):
-        near_copy(jnp.where(lower == 0, late, early)).start()
+    pl.semaphore_wait(barrier, n_member - 1 + rim_sends - jnp.where(first_end, 1, 0))
+
+    @pl.when(last_end)
+    def _():
+        pl.semaphore_signal(far_ready, inc=1, device_id=(r, far), device_id_type=MESH)
+
+    turns = [jnp.where(lower == 0, late, early) for late, early in zip(peers + [far], [far] + peers)]
+    for e in turns[:-1]:
+        near_copy(e).start()
+
+    @pl.when(jnp.logical_not(first_end))
+    def _():
+        near_copy(turns[-1]).start()
 
     @pl.when(to_high)
     def _():
@@ -299,7 +316,7 @@
             h2 = h + h
             for b in range(TILE // SUB):
                 at = pl.ds(b * SUB, SUB)
-                near, image, full, mirror = [
+                near, image, c, full, mirror = [
                     planes[(b * PLANES + p) * SUB :][:SUB, side * TILE : (side + 1) * TILE]
                     for p in range(PLANES)
                 ]
@@ -312,7 +329,7 @@
                 w3 = w * w * w
                 p2 = p * p
                 p3 = p2 * p
-                cp3 = (h2 * x3) * p3
+                cp3 = c * p3
                 alpha = (w + w3) - (p + cp3)
                 gamma = cp3 * p2 * mirror
                 both = full * (w3 - p3) + gamma
@@ -349,6 +366,11 @@
 
     found[...] = find(0)
 
+    @pl.when(first_end)
+    def _():
+        pl.semaphore_wait(far_ready, 1)
+        near_copy(far).start()
+
     @pl.when(has_low)
     def _():
         sized(block(0, half), local_sem.at[0], data_sem.at[1]).wait_recv()
@@ -362,7 +384,9 @@
     sized(block(0, n_member - 1), local_sem.at[0], data_sem.at[0]).wait_recv()
 
     for e in others:
-        tabulate((half + e) * tiles, 1)
+        for t in range(tiles):
+            at = (half + e) * tiles + t
+            sources[at] = source_table(ext[at], middle)
 
     zeros = jnp.zeros((VROWS - 3, TILE), jnp.float32)
 
@@ -532,6 +556,7 @@
             pltpu.VMEM((ROWS, seats), jnp.float32),
             pltpu.SemaphoreType.DMA((7,)),
             pltpu.SemaphoreType.DMA((4,)),
+            pltpu.SemaphoreType.REGULAR,
         ],
         compiler_params=pltpu.CompilerParams(collective_id=0, has_side_effects=True),
     )(

time: 13.3 us -> 13.2 us (level)
  Pallas kernels: 12.2 us -> 12 us
    pallas_call x1, Pallas kernels: 11.5 us -> 11.4 us  [on_device(): pl.pallas_call(functools.partial(kernel, n_region, n_member, pb, own_plat...]
where the time goes in v5:
time: 13.2 us; the launch traced here: 13 us
  Pallas kernels  12 us (91%)
  between operations  0.66 us (5%)
  matrix products  0.36 us (3%)
    pallas_call x1, Pallas kernels, on_device(): pl.pallas_call(functools.partial(kernel, n_region, n_member, pb, own_plat...  11.4 us
    pallas_call x1, Pallas kernels, on_device(): pl.pallas_call(finish, out_shape=(jax.ShapeDtypeStruct(velocity.shape, jn...  0.62 us
    dot_general x1, matrix products, on_device(): jnp.einsum('pab,pb->pa', pre, body_in, preferred_element_type=jnp.float32)  0.36 us

profile of v5, /device:TPU:0, one launch (start us, length us, event | category | flops | bytes accessed | tf_op | source)
XLA Modules:
  0.0 13.0 jit_solution(302953641627267211)
XLA Ops:
  0.6 0.0 copy-start
  0.6 11.4 %shard_map.95 = (f32[3,384]{1,0:T(4,128)S(1)}, bf16[2,486]{1,0:T(2,128)(2,1)S(1)}) custom-call(f32[3,384]{1,0:T(4,128)} %pos_hbm.1, f32[3,384]{1,0:T(4,128)} %force_hbm.1, s32[384]{0:T(512)} %plate_hbm.1, s32[384]{0:T(512)} %rank_hbm.1, s32[8]{0:T(128)} %owner_hbm.1, s32[3,8]{1,0:T(4,128)} %list_hbm.1, s32[3]{0:T(128)} %count_hbm.1), custom_call_target="tpu_custom_call" | custom-call | tf_op jit(solution)/shard_map/pallas_call | solution.py:532
  12.1 0.0 copy-done
  12.1 0.4 %fusion = f32[2,1,486]{2,1,0:T(1,128)S(1)} fusion(bf16[2,486,486]{2,0,1:T(2,128)(2,1)S(1)} %copy-done, bf16[2,486,1]{1,0,2:T(2,128)(2,1)S(1)} %bitcast.5), kind=kOutput, calls=%fused_computation | convolution fusion | flops 944784 | bytes 950616 | tf_op jit(solution)/shard_map/pab,pb->pa/dot_general | solution.py:571
  12.4 0.6 %shard_map.96 = (f32[3,384]{1,0:T(4,128)}, f32[2,486]{1,0:T(2,128)}) custom-call(f32[3,384]{1,0:T(4,128)S(1)} %get-tuple-element.4.vel_ref, f32[2,486]{1,0:T(2,128)S(1)} %bitcast.4), custom_call_target="tpu_custom_call" | custom-call | tf_op jit(solution)/shard_map/pallas_call | solution.py:572
  (1 shorter events, 0.0 us)
Async XLA Ops:
  0.6 11.4 %copy-start = (bf16[2,486,486]{2,0,1:T(2,128)(2,1)S(1)}, bf16[2,486,486]{2,0,1:T(2,128)(2,1)}, u32[]{:S(2)}) copy-start(bf16[2,486,486]{2,0,1:T(2,128)(2,1)} %param.15) | copy-start | bytes 2834356

commit v6 on v5

--- a/solution.py
+++ b/solution.py
@@ -17,6 +17,32 @@
 GATHER = 7
 SCALE = 1.0 / (8.0 * math.pi)
 MESH = pl.DeviceIdType.MESH
+
+
+def pair_terms(x1, x2, x3, src):
+    y1, y2, h, f1, f2, f3, h2 = src
+    d1 = x1 - y1
+    d2 = x2 - y2
+    d3 = x3 - h
+    r3 = x3 + h
+    s = d1 * d1 + d2 * d2
+    w = lax.rsqrt(s + d3 * d3 + 1.0)
+    p = lax.rsqrt(s + r3 * r3)
+    w3 = w * w * w
+    p2 = p * p
+    p3 = p2 * p
+    along = d1 * f1 + d2 * f2
+    full = along + d3 * f3
+    mirror = along - r3 * f3
+    cp3 = (h2 * x3) * p3
+    alpha = (w + w3) - (p + cp3)
+    gamma = 3.0 * (cp3 * p2) * mirror
+    both = full * (w3 - p3) + gamma
+    return (
+        f1 * alpha + d1 * both,
+        f2 * alpha + d2 * both,
+        f3 * alpha + d3 * both + h2 * gamma,
+    )
 
 
 def split3(v):
@@ -307,7 +333,7 @@
             tgt[t * 3 + c] = jnp.broadcast_to(own[c : c + 1], (TILE, TILE)).T
         targets[t] = target_table(own - middle[:3])
 
-    def some_pairs(t, tile_ids, first):
+    def some_pairs(t, tile_ids):
         columns = jnp.concatenate([sources[e] for e in tile_ids], axis=1)
         planes = jnp.dot(targets[t], columns, preferred_element_type=jnp.float32)
         for side, e in enumerate(tile_ids):
@@ -335,14 +361,18 @@
                 both = full * (w3 - p3) + gamma
                 terms = (f1 * alpha + d1 * both, f2 * alpha + d2 * both, f3 * alpha + d3 * both + h2 * gamma)
                 for k in range(3):
-                    if first:
-                        acc[t * 3 + k, at] = terms[k]
-                    else:
-                        acc[t * 3 + k, at] = acc[t * 3 + k, at] + terms[k]
+                    acc[t * 3 + k, at] = acc[t * 3 + k, at] + terms[k]
 
     @pl.loop(0, tiles)
     def _(t):
-        some_pairs(t, [base + t], True)
+        rows = ext[base + t]
+        y1, y2, h, f1, f2, f3 = [jnp.broadcast_to(rows[c : c + 1], (SUB, TILE)) for c in range(6)]
+        source = (y1, y2, h, f1, f2, f3, h + h)
+        for b in range(TILE // SUB):
+            at = pl.ds(b * SUB, SUB)
+            terms = pair_terms(tgt[t * 3, at], tgt[t * 3 + 1, at], tgt[t * 3 + 2, at], source)
+            for k in range(3):
+                acc[t * 3 + k, at] = terms[k]
 
     first_id = (m * (own_plates * pb)).astype(jnp.float32)
     place = lax.broadcasted_iota(jnp.int32, (hot.shape[1], TILE), 0).astype(jnp.float32)
@@ -397,7 +427,7 @@
     for t in range(tiles):
         for s in range(1, pairs, 2):
             chosen = [jnp.where(k < count_ref[t], list_ref[t, k], last) for k in range(s, min(s + 2, pairs))]
-            some_pairs(t, chosen, False)
+            some_pairs(t, chosen)
         blocks.append([jnp.sum(acc[t * 3 + c].T, axis=0, keepdims=True) for c in range(3)] + [zeros])
     rows = jnp.concatenate([jnp.concatenate(block, axis=0) for block in blocks], axis=1)
     vel[m] = rows

time: 13.2 us -> 13.2 us (level)
  no operation moved by 1% of the time
where the time goes in v6:
time: 13.2 us; the launch traced here: 13.1 us
  Pallas kernels  12 us (91%)
  between operations  0.66 us (5%)
  matrix products  0.36 us (3%)
    pallas_call x1, Pallas kernels, on_device(): pl.pallas_call(functools.partial(kernel, n_region, n_member, pb, own_plat...  11.4 us
    pallas_call x1, Pallas kernels, on_device(): pl.pallas_call(finish, out_shape=(jax.ShapeDtypeStruct(velocity.shape, jn...  0.62 us
    dot_general x1, matrix products, on_device(): jnp.einsum('pab,pb->pa', pre, body_in, preferred_element_type=jnp.float32)  0.36 us

profile of v6, /device:TPU:0, one launch (start us, length us, event | category | flops | bytes accessed | tf_op | source)
XLA Modules:
  0.0 13.1 jit_solution(3426100088488726066)
XLA Ops:
  0.6 0.0 copy-start
  0.6 11.4 %shard_map.95 = (f32[3,384]{1,0:T(4,128)S(1)}, bf16[2,486]{1,0:T(2,128)(2,1)S(1)}) custom-call(f32[3,384]{1,0:T(4,128)} %pos_hbm.1, f32[3,384]{1,0:T(4,128)} %force_hbm.1, s32[384]{0:T(512)} %plate_hbm.1, s32[384]{0:T(512)} %rank_hbm.1, s32[8]{0:T(128)} %owner_hbm.1, s32[3,8]{1,0:T(4,128)} %list_hbm.1, s32[3]{0:T(128)} %count_hbm.1), custom_call_target="tpu_custom_call" | custom-call | tf_op jit(solution)/shard_map/pallas_call | solution.py:562
  12.1 0.0 copy-done
  12.1 0.4 %fusion = f32[2,1,486]{2,1,0:T(1,128)S(1)} fusion(bf16[2,486,486]{2,0,1:T(2,128)(2,1)S(1)} %copy-done, bf16[2,486,1]{1,0,2:T(2,128)(2,1)S(1)} %bitcast.5), kind=kOutput, calls=%fused_computation | convolution fusion | flops 944784 | bytes 950616 | tf_op jit(solution)/shard_map/pab,pb->pa/dot_general | solution.py:601
  12.4 0.6 %shard_map.96 = (f32[3,384]{1,0:T(4,128)}, f32[2,486]{1,0:T(2,128)}) custom-call(f32[3,384]{1,0:T(4,128)S(1)} %get-tuple-element.4.vel_ref, f32[2,486]{1,0:T(2,128)S(1)} %bitcast.4), custom_call_target="tpu_custom_call" | custom-call | tf_op jit(solution)/shard_map/pallas_call | solution.py:602
  (1 shorter events, 0.0 us)
Async XLA Ops:
  0.6 11.4 %copy-start = (bf16[2,486,486]{2,0,1:T(2,128)(2,1)S(1)}, bf16[2,486,486]{2,0,1:T(2,128)(2,1)}, u32[]{:S(2)}) copy-start(bf16[2,486,486]{2,0,1:T(2,128)(2,1)} %param.15) | copy-start | bytes 2834356

commit v7 on v6

--- a/solution.py
+++ b/solution.py
@@ -409,8 +409,8 @@
     def _():
         sized(block(0, half), local_sem.at[0], data_sem.at[2]).wait_recv()
 
-    tabulate(0, half)
-    tabulate((half + n_member) * tiles, half)
+    for at in [*range(half * tiles), *range((half + n_member) * tiles, 2 * n_member * tiles)]:
+        sources[at] = source_table(ext[at], middle)
     sized(block(0, n_member - 1), local_sem.at[0], data_sem.at[0]).wait_recv()
 
     for e in others:

time: 13.2 us -> 13.2 us (level)
  no operation moved by 1% of the time
where the time goes in v7:
time: 13.2 us; the launch traced here: 13.1 us
  Pallas kernels  12 us (91%)
  between operations  0.66 us (5%)
  matrix products  0.36 us (3%)
    pallas_call x1, Pallas kernels, on_device(): pl.pallas_call(functools.partial(kernel, n_region, n_member, pb, own_plat...  11.4 us
    pallas_call x1, Pallas kernels, on_device(): pl.pallas_call(finish, out_shape=(jax.ShapeDtypeStruct(velocity.shape, jn...  0.62 us
    dot_general x1, matrix products, on_device(): jnp.einsum('pab,pb->pa', pre, body_in, preferred_element_type=jnp.float32)  0.36 us

profile of v7, /device:TPU:0, one launch (start us, length us, event | category | flops | bytes accessed | tf_op | source)
XLA Modules:
  0.0 13.1 jit_solution(12262679829938291614)
XLA Ops:
  0.6 0.0 copy-start
  0.6 11.4 %shard_map.95 = (f32[3,384]{1,0:T(4,128)S(1)}, bf16[2,486]{1,0:T(2,128)(2,1)S(1)}) custom-call(f32[3,384]{1,0:T(4,128)} %pos_hbm.1, f32[3,384]{1,0:T(4,128)} %force_hbm.1, s32[384]{0:T(512)} %plate_hbm.1, s32[384]{0:T(512)} %rank_hbm.1, s32[8]{0:T(128)} %owner_hbm.1, s32[3,8]{1,0:T(4,128)} %list_hbm.1, s32[3]{0:T(128)} %count_hbm.1), custom_call_target="tpu_custom_call" | custom-call | tf_op jit(solution)/shard_map/pallas_call | solution.py:562
  12.1 0.0 copy-done
  12.1 0.4 %fusion = f32[2,1,486]{2,1,0:T(1,128)S(1)} fusion(bf16[2,486,486]{2,0,1:T(2,128)(2,1)S(1)} %copy-done, bf16[2,486,1]{1,0,2:T(2,128)(2,1)S(1)} %bitcast.5), kind=kOutput, calls=%fused_computation | convolution fusion | flops 944784 | bytes 950616 | tf_op jit(solution)/shard_map/pab,pb->pa/dot_general | solution.py:601
  12.4 0.6 %shard_map.96 = (f32[3,384]{1,0:T(4,128)}, f32[2,486]{1,0:T(2,128)}) custom-call(f32[3,384]{1,0:T(4,128)S(1)} %get-tuple-element.4.vel_ref, f32[2,486]{1,0:T(2,128)S(1)} %bitcast.4), custom_call_target="tpu_custom_call" | custom-call | tf_op jit(solution)/shard_map/pallas_call | solution.py:602
  (1 shorter events, 0.0 us)
Async XLA Ops:
  0.6 11.4 %copy-start = (bf16[2,486,486]{2,0,1:T(2,128)(2,1)S(1)}, bf16[2,486,486]{2,0,1:T(2,128)(2,1)}, u32[]{:S(2)}) copy-start(bf16[2,486,486]{2,0,1:T(2,128)(2,1)} %param.15) | copy-start | bytes 2834356
